TPU v7x, 32 devices: a whole 2x2x4 slice. The times are simulated.
32 devices in a mesh: dp: 2 (over x), expert: 16 (over z, y, core).
Axes of the slice: x: 2, y: 2, z: 4, core: 2. Of those that a mesh axis runs over, the one named last changes fastest.
Arguments:
- tokens: bfloat16 [4096, 2048], P(('dp', 'expert')), may hold values from -6 to 6
- gate_weights: float32 [4096, 2], P(('dp', 'expert')), may hold values from 0.02 to 0.5
- expert_ids: int32 [4096, 2], P(('dp', 'expert')), may hold values from 0 to 15, as said below
- hot_experts: int32 [4], replicated, may hold values from 0 to 15, as said below
- gate_proj: bfloat16 [16, 2048, 768], P('expert', 'dp'), may hold values from -0.125 to 0.125
- up_proj: bfloat16 [16, 2048, 768], P('expert', 'dp'), may hold values from -0.125 to 0.125
- down_proj: bfloat16 [16, 2048, 768], P('expert', 'dp'), may hold values from -0.21875 to 0.21875
- out_grad: bfloat16 [4096, 2048], P(('dp', 'expert')), may hold values from -6 to 6
Outputs:
- layer_out: bfloat16 [4096, 2048], P(('dp', 'expert'))
- tokens_grad: bfloat16 [4096, 2048], P(('dp', 'expert'))
- routing_grad: float32 [4096, 2], P(('dp', 'expert'))
- gate_proj_grad: bfloat16 [16, 2048, 768], P('expert', 'dp')
- up_proj_grad: bfloat16 [16, 2048, 768], P('expert', 'dp')
- down_proj_grad: bfloat16 [16, 2048, 768], P('expert', 'dp')
Inputs may be any that keep to these rules, and one draw needn't show every extreme that they name: `expert_ids`: each token names 2 different experts. In each block of 128 rows of one device no expert is named more than 28 times, and the expert hot_experts[0] is named exactly 28 times in every block. `hot_experts`: 4 different experts.
All inputs are finite; a program needn't handle non-finite values.
Results may differ from a plain program's by a relative error of at most 0.012.
Values may be sent and summed in bfloat16 or wider, within the bound.
No kernel may reach another device: no remote copies, remote signals or barrier semaphores. Data moves between devices by JAX's collectives and lax.ppermute only.
A program may use at most 128 MiB of HBM per device.

v0:
```python
import jax
import jax.numpy as jnp
from jax import lax
from jax.sharding import PartitionSpec as P


TOPK = 2
AXES = ("dp", "expert")


def contract_last(left_side, right_side):
    return lax.dot_general(
        left_side, right_side, (((1,), (1,)), ((), ())), preferred_element_type=jnp.float32
    )


def contract_first(left_side, right_side):
    return lax.dot_general(
        left_side, right_side, (((0,), (0,)), ((), ())), preferred_element_type=jnp.float32
    )


def dot(left_side, right_side):
    return jnp.dot(left_side, right_side, preferred_element_type=jnp.float32)


def make_body(n_dp, n_ex):
    def physical(v, e):
        return ((v >> 1) * 2 + (e & 1)) * n_ex + (e >> 1) * 2 + (v & 1)

    def move(value, where):
        pairs = [
            (physical(v, e), physical(*where(v, e))) for v in range(n_dp) for e in range(n_ex)
        ]
        return lax.ppermute(value, AXES, pairs)

    def transpose(value):
        pairs = [
            (i * n_ex + c, ((i & ~1) | (c & 1)) * n_ex + ((c & ~1) | (i & 1)))
            for i in range(n_dp)
            for c in range(n_ex)
            if (i & 1) != (c & 1)
        ]
        moved = lax.ppermute(value, AXES, pairs)
        stays = (lax.axis_index("dp") & 1) == (lax.axis_index("expert") & 1)
        return lax.optimization_barrier(jnp.where(stays, value, moved))

    half = n_ex // 2

    def across(value):
        return move(value, lambda v, e: (v, e ^ half))

    def to_owner(value, d):
        return move(value, lambda v, e: (v, e ^ d))

    def to_part(value, s):
        return move(value, lambda v, e: (v ^ s, e))

    def body(
        tokens, gate_weights, expert_ids, hot_experts, gate_proj, up_proj, down_proj, out_grad
    ):
        token_count, model_width = tokens.shape
        width = model_width // n_dp
        assign_count = token_count * TOPK
        cap_rows = 5 * assign_count // (4 * n_ex)
        slot_count = cap_rows + assign_count // (2 * n_ex)
        i_index = lax.axis_index("dp")
        c_index = lax.axis_index("expert")
        v_index = (i_index >> 1) * 2 + (c_index & 1)
        e_index = (c_index >> 1) * 2 + (i_index & 1)

        def turn(value):
            cols = [value[:, s * width : (s + 1) * width] for s in range(n_dp)]
            turned = []
            for s in range(n_dp):
                pick = cols[s]
                for j in range(n_dp):
                    if j != s:
                        pick = jnp.where(v_index == (j ^ s), cols[j], pick)
                turned.append(pick)
            return jnp.concatenate(turned, axis=1)

        tok = turn(tokens)
        og = turn(out_grad)
        tok_far = across(tok)
        og_far = across(og)
        tok_two = jnp.concatenate([tok, tok_far], axis=0)
        og_two = jnp.concatenate([og, og_far], axis=0)

        def gathered(shard):
            own = transpose(shard[0])
            return [own] + [to_part(own, s) for s in range(1, n_dp)]

        gate_parts = gathered(gate_proj)
        up_parts = gathered(up_proj)
        down_parts = gathered(down_proj)

        ids = expert_ids.T
        order = jnp.arange(token_count, dtype=jnp.int32)[None, :] * TOPK + jnp.arange(
            TOPK, dtype=jnp.int32
        )[:, None]
        flat_ids = ids.reshape(-1)
        flat_order = order.reshape(-1)
        same = (flat_ids[:, None] == flat_ids[None, :]) & (
            flat_order[:, None] < flat_order[None, :]
        )
        slot_pos = jnp.sum(same.astype(jnp.int32), axis=0)
        hot_row = jnp.any(flat_ids[None, :] == hot_experts[:, None], axis=0)
        kept_mask = slot_pos < jnp.where(hot_row, slot_count, cap_rows)
        target = jnp.where(kept_mask, flat_ids * slot_count + slot_pos, -1)
        routes = jnp.concatenate(
            [target.astype(jnp.float32).reshape(TOPK, -1), gate_weights.T], axis=0
        )
        routes_far = across(routes)
        routes = jnp.concatenate([routes, routes_far], axis=1)
        target_two = routes[:TOPK].astype(jnp.int32)
        weight_two = routes[TOPK:]

        row_count = half * 2 * slot_count
        row = jnp.arange(row_count, dtype=jnp.int32)
        row_d = row // (2 * slot_count)
        row_block = (row // slot_count) % 2
        row_slot = row % slot_count
        row_expert = (e_index // half) * half + ((e_index % half) ^ row_d)
        row_code = row_expert * slot_count + row_slot
        col_block = jnp.arange(2 * token_count, dtype=jnp.int32) // token_count
        row_code = row_code[:, None]
        col_ok = row_block[:, None] == col_block[None, :]
        hits = [(row_code == target_two[k][None, :]) & col_ok for k in range(TOPK)]
        placing = (hits[0] | hits[1]).astype(jnp.bfloat16)
        weighted = jnp.where(
            hits[0], weight_two[0][None, :], jnp.where(hits[1], weight_two[1][None, :], 0.0)
        )
        row_weight = jnp.sum(weighted, axis=1, keepdims=True)
        placing, weighted, row_weight = lax.optimization_barrier(
            (placing, weighted.astype(jnp.bfloat16), row_weight)
        )

        chunk = 2 * slot_count

        def exchange(rows):
            pieces = [rows[d * chunk : (d + 1) * chunk] for d in range(half)]
            moved = [to_owner(pieces[d], d) for d in range(1, half)]
            return jnp.concatenate([pieces[0]] + moved, axis=0)

        tok_rows = dot(placing, tok_two).astype(jnp.bfloat16)
        og_rows = (row_weight * dot(placing, og_two)).astype(jnp.bfloat16)
        expert_rows = exchange(tok_rows)
        grad_in = exchange(og_rows)

        def cols(value, s):
            return value[:, s * width : (s + 1) * width]

        def through(value, parts):
            total = dot(cols(value, 0), parts[0])
            for s in range(1, n_dp):
                total = total + dot(cols(value, s), parts[s])
            return total

        gate_act = through(expert_rows, gate_parts)
        up_act = through(expert_rows, up_parts)
        hidden = (gate_act * jax.nn.sigmoid(gate_act) * up_act).astype(jnp.bfloat16)
        gate_act, up_act, hidden = lax.optimization_barrier((gate_act, up_act, hidden))
        output = jnp.concatenate(
            [contract_last(hidden, part).astype(jnp.bfloat16) for part in down_parts], axis=1
        )
        sigmoid_act = jax.nn.sigmoid(gate_act)
        silu_act = gate_act * sigmoid_act
        returned = exchange(output)

        grad_hidden = through(grad_in, down_parts)
        grad_up = (grad_hidden * silu_act).astype(jnp.bfloat16)
        grad_gate = (
            grad_hidden * up_act * sigmoid_act * (1.0 + gate_act * (1.0 - sigmoid_act))
        ).astype(jnp.bfloat16)
        grad_rows = jnp.concatenate(
            [
                (
                    contract_last(grad_gate, gate_parts[s]) + contract_last(grad_up, up_parts[s])
                ).astype(jnp.bfloat16)
                for s in range(n_dp)
            ],
            axis=1,
        )
        grad_back = exchange(grad_rows)

        def weight_grad(left_side, right_side):
            terms = [
                contract_first(cols(left_side, s), right_side).astype(jnp.bfloat16)
                for s in range(1, n_dp)
            ]
            terms = [to_part(terms[s - 1], s) for s in range(1, n_dp)]
            total = contract_first(cols(left_side, 0), right_side)
            for term in terms:
                total = total + term.astype(jnp.float32)
            return transpose(total.astype(jnp.bfloat16))[None]

        down_proj_grad = weight_grad(grad_in, hidden)
        gate_proj_grad = weight_grad(expert_rows, grad_gate)
        up_proj_grad = weight_grad(expert_rows, grad_up)

        def join(left_side, right_side):
            part = contract_first(left_side, right_side)
            own, other = part[:token_count], part[token_count:].astype(jnp.bfloat16)
            other = across(other)
            return turn((own + other.astype(jnp.float32)).astype(jnp.bfloat16))

        layer_out = join(weighted, returned)
        tokens_grad = join(placing, grad_back)
        inner = contract_last(returned, og_two)
        routing = jnp.stack([jnp.sum(jnp.where(hit, inner, 0.0), axis=0) for hit in hits])
        routing_grad = (routing[:, :token_count] + across(routing[:, token_count:])).T
        return (layer_out, tokens_grad, routing_grad, gate_proj_grad, up_proj_grad, down_proj_grad)

    return body


def solution(mesh):
    in_specs = (
        P(("dp", "expert"), None),
        P(("dp", "expert"), None),
        P(("dp", "expert"), None),
        P(),
        P("expert", "dp", None),
        P("expert", "dp", None),
        P("expert", "dp", None),
        P(("dp", "expert"), None),
    )
    out_specs = (
        P(("dp", "expert"), None),
        P(("dp", "expert"), None),
        P(("dp", "expert"), None),
        P("expert", "dp", None),
        P("expert", "dp", None),
        P("expert", "dp", None),
    )
    body = make_body(mesh.shape["dp"], mesh.shape["expert"])
    return jax.shard_map(body, mesh=mesh, in_specs=in_specs, out_specs=out_specs, check_vma=False)
```

profile of v0, /device:TPU:13, one launch (start us, length us, event | category | flops | bytes accessed | tf_op | source)
XLA Modules:
  0.0 294.1 jit_solution(1637990455059512587)
XLA Ops:
  3.7 2.3 collective-permute-start
  9.0 2.4 collective-permute-start.1
  11.4 4.5 %collective-permute-start.11 = (bf16[1024,768]{1,0:T(8,128)(2,1)S(1)}, bf16[1024,768]{1,0:T(8,128)(2,1)}, u32[]{:S(2)}, u32[]{:S(2)}) collective-permute-start(bf16[1024,768]{1,0:T(8,128)(2,1)S(1)} %bitcast.66), channel_id=1, source_target_pairs={{1,16},{3,18},{5,20},{7,22},{9,24},{11,26},{13,28},{15,30},{16,1},... | collective-permute-start | bytes 4718600 | tf_op jit(solution)/shard_map/ppermute | solution.py:44
  15.9 1.9 collective-permute-start.9
  17.9 3.6 %collective-permute-start.13 = (bf16[1024,768]{1,0:T(8,128)(2,1)}, bf16[1024,768]{1,0:T(8,128)(2,1)S(1)}, u32[]{:S(2)}, u32[]{:S(2)}) collective-permute-start(bf16[1024,768]{1,0:T(8,128)(2,1)} %bitcast.68), channel_id=1, source_target_pairs={{1,16},{3,18},{5,20},{7,22},{9,24},{11,26},{13,28},{15,30},{16,1},... | collective-permute-start | bytes 4718600 | tf_op jit(solution)/shard_map/ppermute | solution.py:44
  22.6 19.8 %collective-permute-done.23 = bf16[128,2048]{1,0:T(8,128)(2,1)} collective-permute-done((bf16[128,2048]{1,0:T(8,128)(2,1)}, bf16[128,2048]{1,0:T(8,128)(2,1)}, u32[]{:S(2)}, u32[]{:S(2)}) %collective-permute-start.23) | collective-permute-done | bytes 524320 | tf_op jit(solution)/shard_map/ppermute | solution.py:35
  42.4 1.8 multiply_convert_fusion
  45.7 8.0 %collective-permute-done.1 = bf16[128,2048]{1,0:T(8,128)(2,1)} collective-permute-done((bf16[128,2048]{1,0:T(8,128)(2,1)}, bf16[128,2048]{1,0:T(8,128)(2,1)}, u32[]{:S(2)}, u32[]{:S(2)}) %collective-permute-start.1) | collective-permute-done | bytes 524320 | tf_op jit(solution)/shard_map/ppermute | solution.py:35
  53.8 1.7 convolution_convert_fusion
  55.7 16.1 %collective-permute-done.24 = bf16[56,2048]{1,0:T(8,128)(2,1)S(1)} collective-permute-done((bf16[56,2048]{1,0:T(8,128)(2,1)S(1)}, bf16[56,2048]{1,0:T(8,128)(2,1)S(1)}, u32[]{:S(2)}, u32[]{:S(2)}) %collective-permute-start.24) | collective-permute-done | bytes 229408 | tf_op jit(solution)/shard_map/ppermute | solution.py:35
  71.8 1.8 collective-permute-start.26
  74.0 4.9 %collective-permute-done.26 = bf16[56,2048]{1,0:T(8,128)(2,1)S(1)} collective-permute-done((bf16[56,2048]{1,0:T(8,128)(2,1)S(1)}, bf16[56,2048]{1,0:T(8,128)(2,1)S(1)}, u32[]{:S(2)}, u32[]{:S(2)}) %collective-permute-start.26) | collective-permute-done | bytes 229408 | tf_op jit(solution)/shard_map/ppermute | solution.py:35
  78.9 2.2 collective-permute-start.28
  81.3 1.7 collective-permute-start.29
  83.0 3.1 %collective-permute-done.28 = bf16[56,2048]{1,0:T(8,128)(2,1)S(1)} collective-permute-done((bf16[56,2048]{1,0:T(8,128)(2,1)S(1)}, bf16[56,2048]{1,0:T(8,128)(2,1)S(1)}, u32[]{:S(2)}, u32[]{:S(2)}) %collective-permute-start.28) | collective-permute-done | bytes 229408 | tf_op jit(solution)/shard_map/ppermute | solution.py:35
  86.1 3.2 %collective-permute-start.30 = (bf16[56,2048]{1,0:T(8,128)(2,1)S(1)}, bf16[56,2048]{1,0:T(8,128)(2,1)S(1)}, u32[]{:S(2)}, u32[]{:S(2)}) collective-permute-start(bf16[56,2048]{1,0:T(8,128)(2,1)S(1)} %get-tuple-element.30), channel_id=1, source_target_pairs={{0,22},{16,6},{2,20},{18,4},{4,18},{20,2},{6,16},{22,0},{8,30},{24... | collective-permute-start | bytes 688136 | tf_op jit(solution)/shard_map/ppermute | solution.py:35
  89.3 5.2 %collective-permute-done.29 = bf16[56,2048]{1,0:T(8,128)(2,1)S(1)} collective-permute-done((bf16[56,2048]{1,0:T(8,128)(2,1)S(1)}, bf16[56,2048]{1,0:T(8,128)(2,1)S(1)}, u32[]{:S(2)}, u32[]{:S(2)}) %collective-permute-start.29) | collective-permute-done | bytes 229408 | tf_op jit(solution)/shard_map/ppermute | solution.py:35
  94.5 1.8 collective-permute-done.30
  97.0 6.1 %collective-permute-done.2 = bf16[56,2048]{1,0:T(8,128)(2,1)S(1)} collective-permute-done((bf16[56,2048]{1,0:T(8,128)(2,1)S(1)}, bf16[56,2048]{1,0:T(8,128)(2,1)S(1)}, u32[]{:S(2)}, u32[]{:S(2)}) %collective-permute-start.2) | collective-permute-done | bytes 229408 | tf_op jit(solution)/shard_map/ppermute | solution.py:35
  103.1 2.7 collective-permute-start.4
  105.9 5.3 %collective-permute-done.4 = bf16[56,2048]{1,0:T(8,128)(2,1)S(1)} collective-permute-done((bf16[56,2048]{1,0:T(8,128)(2,1)S(1)}, bf16[56,2048]{1,0:T(8,128)(2,1)S(1)}, u32[]{:S(2)}, u32[]{:S(2)}) %collective-permute-start.4) | collective-permute-done | bytes 229408 | tf_op jit(solution)/shard_map/ppermute | solution.py:35
  111.9 2.7 collective-permute-start.7
  118.5 1.6 collective-permute-start.8
  120.1 3.6 %collective-permute-done.7 = bf16[56,2048]{1,0:T(8,128)(2,1)S(1)} collective-permute-done((bf16[56,2048]{1,0:T(8,128)(2,1)S(1)}, bf16[56,2048]{1,0:T(8,128)(2,1)S(1)}, u32[]{:S(2)}, u32[]{:S(2)}) %collective-permute-start.7) | collective-permute-done | bytes 229408 | tf_op jit(solution)/shard_map/ppermute | solution.py:35
  123.8 4.8 %collective-permute-done.8 = bf16[56,2048]{1,0:T(8,128)(2,1)S(1)} collective-permute-done((bf16[56,2048]{1,0:T(8,128)(2,1)S(1)}, bf16[56,2048]{1,0:T(8,128)(2,1)S(1)}, u32[]{:S(2)}, u32[]{:S(2)}) %collective-permute-start.8) | collective-permute-done | bytes 229408 | tf_op jit(solution)/shard_map/ppermute | solution.py:35
  128.8 2.4 collective-permute-start.14
  149.3 1.9 collective-permute-done.15
  151.2 1.6 collective-permute-start.17
  152.9 5.0 %collective-permute-done.17 = bf16[56,2048]{1,0:T(8,128)(2,1)S(1)} collective-permute-done((bf16[56,2048]{1,0:T(8,128)(2,1)S(1)}, bf16[56,2048]{1,0:T(8,128)(2,1)S(1)}, u32[]{:S(2)}, u32[]{:S(2)}) %collective-permute-start.17) | collective-permute-done | bytes 229408 | tf_op jit(solution)/shard_map/ppermute | solution.py:35
  158.5 2.4 collective-permute-start.20
  160.9 2.8 collective-permute-done.19
  164.3 4.7 %collective-permute-done.20 = bf16[56,2048]{1,0:T(8,128)(2,1)S(1)} collective-permute-done((bf16[56,2048]{1,0:T(8,128)(2,1)S(1)}, bf16[56,2048]{1,0:T(8,128)(2,1)S(1)}, u32[]{:S(2)}, u32[]{:S(2)}) %collective-permute-start.20) | collective-permute-done | bytes 229408 | tf_op jit(solution)/shard_map/ppermute | solution.py:35
  169.5 4.3 %collective-permute-done.21 = bf16[56,2048]{1,0:T(8,128)(2,1)S(1)} collective-permute-done((bf16[56,2048]{1,0:T(8,128)(2,1)S(1)}, bf16[56,2048]{1,0:T(8,128)(2,1)S(1)}, u32[]{:S(2)}, u32[]{:S(2)}) %collective-permute-start.21) | collective-permute-done | bytes 229408 | tf_op jit(solution)/shard_map/ppermute | solution.py:35
  175.5 1.8 select_reduce_fusion.1
  177.4 1.8 collective-permute-start.33
  179.5 3.8 %collective-permute-done.33 = bf16[56,2048]{1,0:T(8,128)(2,1)S(1)} collective-permute-done((bf16[56,2048]{1,0:T(8,128)(2,1)S(1)}, bf16[56,2048]{1,0:T(8,128)(2,1)S(1)}, u32[]{:S(2)}, u32[]{:S(2)}) %collective-permute-start.33) | collective-permute-done | bytes 229408 | tf_op jit(solution)/shard_map/ppermute | solution.py:35
  184.6 1.7 collective-permute-start.36
  186.3 3.1 %collective-permute-done.35 = bf16[56,2048]{1,0:T(8,128)(2,1)S(1)} collective-permute-done((bf16[56,2048]{1,0:T(8,128)(2,1)S(1)}, bf16[56,2048]{1,0:T(8,128)(2,1)S(1)}, u32[]{:S(2)}, u32[]{:S(2)}) %collective-permute-start.35) | collective-permute-done | bytes 229408 | tf_op jit(solution)/shard_map/ppermute | solution.py:35
  190.3 3.2 %collective-permute-done.36 = bf16[56,2048]{1,0:T(8,128)(2,1)S(1)} collective-permute-done((bf16[56,2048]{1,0:T(8,128)(2,1)S(1)}, bf16[56,2048]{1,0:T(8,128)(2,1)S(1)}, u32[]{:S(2)}, u32[]{:S(2)}) %collective-permute-start.36) | collective-permute-done | bytes 229408 | tf_op jit(solution)/shard_map/ppermute | solution.py:35
  193.6 4.9 %collective-permute-done.37 = bf16[56,2048]{1,0:T(8,128)(2,1)S(1)} collective-permute-done((bf16[56,2048]{1,0:T(8,128)(2,1)S(1)}, bf16[56,2048]{1,0:T(8,128)(2,1)S(1)}, u32[]{:S(2)}, u32[]{:S(2)}) %collective-permute-start.37) | collective-permute-done | bytes 229408 | tf_op jit(solution)/shard_map/ppermute | solution.py:35
  199.4 2.4 collective-permute-start.38
  202.4 25.7 %collective-permute-done.22 = bf16[128,2048]{1,0:T(8,128)(2,1)S(1)} collective-permute-done((bf16[128,2048]{1,0:T(8,128)(2,1)S(1)}, bf16[128,2048]{1,0:T(8,128)(2,1)S(1)}, u32[]{:S(2)}, u32[]{:S(2)}) %collective-permute-start.22) | collective-permute-done | bytes 524320 | tf_op jit(solution)/shard_map/ppermute | solution.py:35
  229.2 11.8 %collective-permute-start.45 = (bf16[1024,768]{1,0:T(8,128)(2,1)S(1)}, bf16[1024,768]{1,0:T(8,128)(2,1)S(1)}, u32[]{:S(2)}, u32[]{:S(2)}) collective-permute-start(bf16[1024,768]{1,0:T(8,128)(2,1)S(1)} %add_convert_fusion), channel_id=1, source_target_pairs={{1,16},{3,18},{5,20},{7,22},{9,24},{11,26},{13,28},{15,30},{16,1},... | collective-permute-start | bytes 4718600 | tf_op jit(solution)/shard_map/ppermute | solution.py:44
  242.0 1.9 collective-permute-start.43
  245.0 3.6 %collective-permute-start.41 = (bf16[1024,768]{1,0:T(8,128)(2,1)S(1)}, bf16[1024,768]{1,0:T(8,128)(2,1)S(1)}, u32[]{:S(2)}, u32[]{:S(2)}) collective-permute-start(bf16[1024,768]{1,0:T(8,128)(2,1)S(1)} %add_convert_fusion.2), channel_id=1, source_target_pairs={{1,16},{3,18},{5,20},{7,22},{9,24},{11,26},{13,28},{15,30},{16,1},... | collective-permute-start | bytes 4718600 | tf_op jit(solution)/shard_map/ppermute | solution.py:44
  250.5 8.5 %collective-permute-done.45 = bf16[1024,768]{1,0:T(8,128)(2,1)S(1)} collective-permute-done((bf16[1024,768]{1,0:T(8,128)(2,1)S(1)}, bf16[1024,768]{1,0:T(8,128)(2,1)S(1)}, u32[]{:S(2)}, u32[]{:S(2)}) %collective-permute-start.45) | collective-permute-done | bytes 1572896 | tf_op jit(solution)/shard_map/ppermute | solution.py:44
  260.4 15.5 %collective-permute-done.43 = bf16[1024,768]{1,0:T(8,128)(2,1)S(1)} collective-permute-done((bf16[1024,768]{1,0:T(8,128)(2,1)S(1)}, bf16[1024,768]{1,0:T(8,128)(2,1)S(1)}, u32[]{:S(2)}, u32[]{:S(2)}) %collective-permute-start.43) | collective-permute-done | bytes 1572896 | tf_op jit(solution)/shard_map/ppermute | solution.py:44
  277.2 15.5 %collective-permute-done.41 = bf16[1024,768]{1,0:T(8,128)(2,1)S(1)} collective-permute-done((bf16[1024,768]{1,0:T(8,128)(2,1)S(1)}, bf16[1024,768]{1,0:T(8,128)(2,1)S(1)}, u32[]{:S(2)}, u32[]{:S(2)}) %collective-permute-start.41) | collective-permute-done | bytes 1572896 | tf_op jit(solution)/shard_map/ppermute | solution.py:44
  (157 shorter events, 49.3 us)
Async XLA Ops:
  3.7 14.2 %collective-permute-start = (f32[4,128]{1,0:T(4,128)S(1)}, f32[4,128]{1,0:T(4,128)S(1)}, u32[]{:S(2)}, u32[]{:S(2)}) collective-permute-start(f32[4,128]{1,0:T(4,128)S(1)} %pad_maximum_fusion.10), channel_id=1, source_target_pairs={{0,8},{16,24},{2,10},{18,26},{4,12},{20,28},{6,14},{22,30},{8,0},{... | collective-permute-start | bytes 6152 | tf_op jit(solution)/shard_map/ppermute | solution.py:35
  7.2 14.4 %copy-start.10 = (f32[128,2]{0,1:T(2,128)S(1)}, f32[128,2]{0,1:T(2,128)}, u32[]{:S(2)}) copy-start(f32[128,2]{0,1:T(2,128)} %param.9) | copy-start | bytes 3076
  8.0 34.4 %collective-permute-start.23 = (bf16[128,2048]{1,0:T(8,128)(2,1)}, bf16[128,2048]{1,0:T(8,128)(2,1)}, u32[]{:S(2)}, u32[]{:S(2)}) collective-permute-start(bf16[128,2048]{1,0:T(8,128)(2,1)} %pad_maximum_fusion.3), channel_id=1, source_target_pairs={{0,8},{16,24},{2,10},{18,26},{4,12},{20,28},{6,14},{22,30},{8,0},{... | collective-permute-start | bytes 1572872 | tf_op jit(solution)/shard_map/ppermute | solution.py:35
  9.0 44.7 %collective-permute-start.1 = (bf16[128,2048]{1,0:T(8,128)(2,1)}, bf16[128,2048]{1,0:T(8,128)(2,1)}, u32[]{:S(2)}, u32[]{:S(2)}) collective-permute-start(bf16[128,2048]{1,0:T(8,128)(2,1)} %pad_maximum_fusion.1), channel_id=1, source_target_pairs={{0,8},{16,24},{2,10},{18,26},{4,12},{20,28},{6,14},{22,30},{8,0},{... | collective-permute-start | bytes 1572872 | tf_op jit(solution)/shard_map/ppermute | solution.py:35
  11.4 100.5 %collective-permute-start.11 = (bf16[1024,768]{1,0:T(8,128)(2,1)S(1)}, bf16[1024,768]{1,0:T(8,128)(2,1)}, u32[]{:S(2)}, u32[]{:S(2)}) collective-permute-start(bf16[1024,768]{1,0:T(8,128)(2,1)S(1)} %bitcast.66), channel_id=1, source_target_pairs={{1,16},{3,18},{5,20},{7,22},{9,24},{11,26},{13,28},{15,30},{16,1},... | collective-permute-start | bytes 4718600 | tf_op jit(solution)/shard_map/ppermute | solution.py:44
  15.9 100.3 %collective-permute-start.9 = (bf16[1024,768]{1,0:T(8,128)(2,1)S(1)}, bf16[1024,768]{1,0:T(8,128)(2,1)}, u32[]{:S(2)}, u32[]{:S(2)}) collective-permute-start(bf16[1024,768]{1,0:T(8,128)(2,1)S(1)} %bitcast.67), channel_id=1, source_target_pairs={{1,16},{3,18},{5,20},{7,22},{9,24},{11,26},{13,28},{15,30},{16,1},... | collective-permute-start | bytes 4718600 | tf_op jit(solution)/shard_map/ppermute | solution.py:44
  17.9 110.6 %collective-permute-start.13 = (bf16[1024,768]{1,0:T(8,128)(2,1)}, bf16[1024,768]{1,0:T(8,128)(2,1)S(1)}, u32[]{:S(2)}, u32[]{:S(2)}) collective-permute-start(bf16[1024,768]{1,0:T(8,128)(2,1)} %bitcast.68), channel_id=1, source_target_pairs={{1,16},{3,18},{5,20},{7,22},{9,24},{11,26},{13,28},{15,30},{16,1},... | collective-permute-start | bytes 4718600 | tf_op jit(solution)/shard_map/ppermute | solution.py:44
  44.4 27.4 %collective-permute-start.24 = (bf16[56,2048]{1,0:T(8,128)(2,1)S(1)}, bf16[56,2048]{1,0:T(8,128)(2,1)S(1)}, u32[]{:S(2)}, u32[]{:S(2)}) collective-permute-start(bf16[56,2048]{1,0:T(8,128)(2,1)S(1)} %get-tuple-element.36), channel_id=1, source_target_pairs={{0,16},{16,0},{2,18},{18,2},{4,20},{20,4},{6,22},{22,6},{8,24},{24... | collective-permute-start | bytes 688136 | tf_op jit(solution)/shard_map/ppermute | solution.py:35
  53.6 20.1 %collective-permute-start.25 = (bf16[56,2048]{1,0:T(8,128)(2,1)S(1)}, bf16[56,2048]{1,0:T(8,128)(2,1)S(1)}, u32[]{:S(2)}, u32[]{:S(2)}) collective-permute-start(bf16[56,2048]{1,0:T(8,128)(2,1)S(1)} %get-tuple-element.35), channel_id=1, source_target_pairs={{0,2},{16,18},{2,0},{18,16},{4,6},{20,22},{6,4},{22,20},{8,10},{24... | collective-permute-start | bytes 688136 | tf_op jit(solution)/shard_map/ppermute | solution.py:35
  71.8 7.0 %collective-permute-start.26 = (bf16[56,2048]{1,0:T(8,128)(2,1)S(1)}, bf16[56,2048]{1,0:T(8,128)(2,1)S(1)}, u32[]{:S(2)}, u32[]{:S(2)}) collective-permute-start(bf16[56,2048]{1,0:T(8,128)(2,1)S(1)} %get-tuple-element.34), channel_id=1, source_target_pairs={{0,18},{16,2},{2,16},{18,0},{4,22},{20,6},{6,20},{22,4},{8,26},{24... | collective-permute-start | bytes 688136 | tf_op jit(solution)/shard_map/ppermute | solution.py:35
  73.7 7.6 %collective-permute-start.27 = (bf16[56,2048]{1,0:T(8,128)(2,1)S(1)}, bf16[56,2048]{1,0:T(8,128)(2,1)S(1)}, u32[]{:S(2)}, u32[]{:S(2)}) collective-permute-start(bf16[56,2048]{1,0:T(8,128)(2,1)S(1)} %get-tuple-element.33), channel_id=1, source_target_pairs={{0,4},{16,20},{2,6},{18,22},{4,0},{20,16},{6,2},{22,18},{8,12},{24... | collective-permute-start | bytes 688136 | tf_op jit(solution)/shard_map/ppermute | solution.py:35
  78.9 7.2 %collective-permute-start.28 = (bf16[56,2048]{1,0:T(8,128)(2,1)S(1)}, bf16[56,2048]{1,0:T(8,128)(2,1)S(1)}, u32[]{:S(2)}, u32[]{:S(2)}) collective-permute-start(bf16[56,2048]{1,0:T(8,128)(2,1)S(1)} %get-tuple-element.32), channel_id=1, source_target_pairs={{0,20},{16,4},{2,22},{18,6},{4,16},{20,0},{6,18},{22,2},{8,28},{24... | collective-permute-start | bytes 688136 | tf_op jit(solution)/shard_map/ppermute | solution.py:35
  81.3 13.2 %collective-permute-start.29 = (bf16[56,2048]{1,0:T(8,128)(2,1)S(1)}, bf16[56,2048]{1,0:T(8,128)(2,1)S(1)}, u32[]{:S(2)}, u32[]{:S(2)}) collective-permute-start(bf16[56,2048]{1,0:T(8,128)(2,1)S(1)} %get-tuple-element.31), channel_id=1, source_target_pairs={{0,6},{16,22},{2,4},{18,20},{4,2},{20,18},{6,0},{22,16},{8,14},{24... | collective-permute-start | bytes 688136 | tf_op jit(solution)/shard_map/ppermute | solution.py:35
  86.1 10.2 %collective-permute-start.30 = (bf16[56,2048]{1,0:T(8,128)(2,1)S(1)}, bf16[56,2048]{1,0:T(8,128)(2,1)S(1)}, u32[]{:S(2)}, u32[]{:S(2)}) collective-permute-start(bf16[56,2048]{1,0:T(8,128)(2,1)S(1)} %get-tuple-element.30), channel_id=1, source_target_pairs={{0,22},{16,6},{2,20},{18,4},{4,18},{20,2},{6,16},{22,0},{8,30},{24... | collective-permute-start | bytes 688136 | tf_op jit(solution)/shard_map/ppermute | solution.py:35
  94.5 8.6 %collective-permute-start.2 = (bf16[56,2048]{1,0:T(8,128)(2,1)S(1)}, bf16[56,2048]{1,0:T(8,128)(2,1)S(1)}, u32[]{:S(2)}, u32[]{:S(2)}) collective-permute-start(bf16[56,2048]{1,0:T(8,128)(2,1)S(1)} %get-tuple-element.52), channel_id=1, source_target_pairs={{0,16},{16,0},{2,18},{18,2},{4,20},{20,4},{6,22},{22,6},{8,24},{24... | collective-permute-start | bytes 688136 | tf_op jit(solution)/shard_map/ppermute | solution.py:35
  96.3 9.4 %collective-permute-start.3 = (bf16[56,2048]{1,0:T(8,128)(2,1)S(1)}, bf16[56,2048]{1,0:T(8,128)(2,1)S(1)}, u32[]{:S(2)}, u32[]{:S(2)}) collective-permute-start(bf16[56,2048]{1,0:T(8,128)(2,1)S(1)} %get-tuple-element.51), channel_id=1, source_target_pairs={{0,2},{16,18},{2,0},{18,16},{4,6},{20,22},{6,4},{22,20},{8,10},{24... | collective-permute-start | bytes 688136 | tf_op jit(solution)/shard_map/ppermute | solution.py:35
  103.1 8.1 %collective-permute-start.4 = (bf16[56,2048]{1,0:T(8,128)(2,1)S(1)}, bf16[56,2048]{1,0:T(8,128)(2,1)S(1)}, u32[]{:S(2)}, u32[]{:S(2)}) collective-permute-start(bf16[56,2048]{1,0:T(8,128)(2,1)S(1)} %get-tuple-element.50), channel_id=1, source_target_pairs={{0,18},{16,2},{2,16},{18,0},{4,22},{20,6},{6,20},{22,4},{8,26},{24... | collective-permute-start | bytes 688136 | tf_op jit(solution)/shard_map/ppermute | solution.py:35
  105.8 12.6 %collective-permute-start.5 = (bf16[56,2048]{1,0:T(8,128)(2,1)S(1)}, bf16[56,2048]{1,0:T(8,128)(2,1)S(1)}, u32[]{:S(2)}, u32[]{:S(2)}) collective-permute-start(bf16[56,2048]{1,0:T(8,128)(2,1)S(1)} %get-tuple-element.49), channel_id=1, source_target_pairs={{0,4},{16,20},{2,6},{18,22},{4,0},{20,16},{6,2},{22,18},{8,12},{24... | collective-permute-start | bytes 688136 | tf_op jit(solution)/shard_map/ppermute | solution.py:35
  111.2 7.3 %collective-permute-start.6 = (bf16[56,2048]{1,0:T(8,128)(2,1)S(1)}, bf16[56,2048]{1,0:T(8,128)(2,1)S(1)}, u32[]{:S(2)}, u32[]{:S(2)}) collective-permute-start(bf16[56,2048]{1,0:T(8,128)(2,1)S(1)} %get-tuple-element.48), channel_id=1, source_target_pairs={{0,20},{16,4},{2,22},{18,6},{4,16},{20,0},{6,18},{22,2},{8,28},{24... | collective-permute-start | bytes 688136 | tf_op jit(solution)/shard_map/ppermute | solution.py:35
  111.9 11.9 %collective-permute-start.7 = (bf16[56,2048]{1,0:T(8,128)(2,1)S(1)}, bf16[56,2048]{1,0:T(8,128)(2,1)S(1)}, u32[]{:S(2)}, u32[]{:S(2)}) collective-permute-start(bf16[56,2048]{1,0:T(8,128)(2,1)S(1)} %get-tuple-element.47), channel_id=1, source_target_pairs={{0,6},{16,22},{2,4},{18,20},{4,2},{20,18},{6,0},{22,16},{8,14},{24... | collective-permute-start | bytes 688136 | tf_op jit(solution)/shard_map/ppermute | solution.py:35
  116.2 15.0 %collective-permute-start.12 = (bf16[1024,768]{1,0:T(8,128)(2,1)S(1)}, bf16[1024,768]{1,0:T(8,128)(2,1)S(1)}, u32[]{:S(2)}, u32[]{:S(2)}) collective-permute-start(bf16[1024,768]{1,0:T(8,128)(2,1)S(1)} %broadcast_select_fusion.4), channel_id=1, source_target_pairs={{0,1},{16,17},{2,3},{18,19},{4,5},{20,21},{6,7},{22,23},{8,9},{24,... | collective-permute-start | bytes 4718600 | tf_op jit(solution)/shard_map/ppermute | solution.py:35
  118.3 10.2 %copy-start.2 = (bf16[1,1024,768]{2,1,0:T(8,128)(2,1)S(1)}, bf16[1,1024,768]{2,1,0:T(8,128)(2,1)}, u32[]{:S(2)}) copy-start(bf16[1,1024,768]{2,1,0:T(8,128)(2,1)} %param.14) | copy-start | bytes 4718596
  118.4 13.7 %collective-permute-start.10 = (bf16[1024,768]{1,0:T(8,128)(2,1)S(1)}, bf16[1024,768]{1,0:T(8,128)(2,1)S(1)}, u32[]{:S(2)}, u32[]{:S(2)}) collective-permute-start(bf16[1024,768]{1,0:T(8,128)(2,1)S(1)} %broadcast_select_fusion.5), channel_id=1, source_target_pairs={{0,1},{16,17},{2,3},{18,19},{4,5},{20,21},{6,7},{22,23},{8,9},{24,... | collective-permute-start | bytes 4718600 | tf_op jit(solution)/shard_map/ppermute | solution.py:35
  118.5 10.1 %collective-permute-start.8 = (bf16[56,2048]{1,0:T(8,128)(2,1)S(1)}, bf16[56,2048]{1,0:T(8,128)(2,1)S(1)}, u32[]{:S(2)}, u32[]{:S(2)}) collective-permute-start(bf16[56,2048]{1,0:T(8,128)(2,1)S(1)} %get-tuple-element.46), channel_id=1, source_target_pairs={{0,22},{16,6},{2,20},{18,4},{4,18},{20,2},{6,16},{22,0},{8,30},{24... | collective-permute-start | bytes 688136 | tf_op jit(solution)/shard_map/ppermute | solution.py:35
  128.8 8.1 %collective-permute-start.14 = (bf16[1024,768]{1,0:T(8,128)(2,1)S(1)}, bf16[1024,768]{1,0:T(8,128)(2,1)S(1)}, u32[]{:S(2)}, u32[]{:S(2)}) collective-permute-start(bf16[1024,768]{1,0:T(8,128)(2,1)S(1)} %broadcast_select_fusion.3), channel_id=1, source_target_pairs={{0,1},{16,17},{2,3},{18,19},{4,5},{20,21},{6,7},{22,23},{8,9},{24,... | collective-permute-start | bytes 4718600 | tf_op jit(solution)/shard_map/ppermute | solution.py:35
  141.5 86.6 %collective-permute-start.44 = (bf16[1024,768]{1,0:T(8,128)(2,1)S(1)}, bf16[1024,768]{1,0:T(8,128)(2,1)S(1)}, u32[]{:S(2)}, u32[]{:S(2)}) collective-permute-start(bf16[1024,768]{1,0:T(8,128)(2,1)S(1)} %convolution_convert_fusion.1), channel_id=1, source_target_pairs={{0,1},{16,17},{2,3},{18,19},{4,5},{20,21},{6,7},{22,23},{8,9},{24,... | collective-permute-start | bytes 4718600 | tf_op jit(solution)/shard_map/ppermute | solution.py:35
  141.6 99.4 %collective-permute-start.42 = (bf16[1024,768]{1,0:T(8,128)(2,1)S(1)}, bf16[1024,768]{1,0:T(8,128)(2,1)S(1)}, u32[]{:S(2)}, u32[]{:S(2)}) collective-permute-start(bf16[1024,768]{1,0:T(8,128)(2,1)S(1)} %convolution_convert_fusion.2), channel_id=1, source_target_pairs={{0,1},{16,17},{2,3},{18,19},{4,5},{20,21},{6,7},{22,23},{8,9},{24,... | collective-permute-start | bytes 4718600 | tf_op jit(solution)/shard_map/ppermute | solution.py:35
  143.1 100.8 %collective-permute-start.40 = (bf16[1024,768]{1,0:T(8,128)(2,1)S(1)}, bf16[1024,768]{1,0:T(8,128)(2,1)S(1)}, u32[]{:S(2)}, u32[]{:S(2)}) collective-permute-start(bf16[1024,768]{1,0:T(8,128)(2,1)S(1)} %convolution_convert_fusion.3), channel_id=1, source_target_pairs={{0,1},{16,17},{2,3},{18,19},{4,5},{20,21},{6,7},{22,23},{8,9},{24,... | collective-permute-start | bytes 4718600 | tf_op jit(solution)/shard_map/ppermute | solution.py:35
  144.4 6.8 %collective-permute-start.15 = (bf16[56,2048]{1,0:T(8,128)(2,1)S(1)}, bf16[56,2048]{1,0:T(8,128)(2,1)S(1)}, u32[]{:S(2)}, u32[]{:S(2)}) collective-permute-start(bf16[56,2048]{1,0:T(8,128)(2,1)S(1)} %get-tuple-element.40), channel_id=1, source_target_pairs={{0,16},{16,0},{2,18},{18,2},{4,20},{20,4},{6,22},{22,6},{8,24},{24... | collective-permute-start | bytes 688136 | tf_op jit(solution)/shard_map/ppermute | solution.py:35
  145.6 7.2 %collective-permute-start.16 = (bf16[56,2048]{1,0:T(8,128)(2,1)S(1)}, bf16[56,2048]{1,0:T(8,128)(2,1)S(1)}, u32[]{:S(2)}, u32[]{:S(2)}) collective-permute-start(bf16[56,2048]{1,0:T(8,128)(2,1)S(1)} %get-tuple-element.41), channel_id=1, source_target_pairs={{0,2},{16,18},{2,0},{18,16},{4,6},{20,22},{6,4},{22,20},{8,10},{24... | collective-permute-start | bytes 688136 | tf_op jit(solution)/shard_map/ppermute | solution.py:35
  151.2 6.8 %collective-permute-start.17 = (bf16[56,2048]{1,0:T(8,128)(2,1)S(1)}, bf16[56,2048]{1,0:T(8,128)(2,1)S(1)}, u32[]{:S(2)}, u32[]{:S(2)}) collective-permute-start(bf16[56,2048]{1,0:T(8,128)(2,1)S(1)} %get-tuple-element.42), channel_id=1, source_target_pairs={{0,18},{16,2},{2,16},{18,0},{4,22},{20,6},{6,20},{22,4},{8,26},{24... | collective-permute-start | bytes 688136 | tf_op jit(solution)/shard_map/ppermute | solution.py:35
  152.8 5.7 %collective-permute-start.18 = (bf16[56,2048]{1,0:T(8,128)(2,1)S(1)}, bf16[56,2048]{1,0:T(8,128)(2,1)S(1)}, u32[]{:S(2)}, u32[]{:S(2)}) collective-permute-start(bf16[56,2048]{1,0:T(8,128)(2,1)S(1)} %get-tuple-element.43), channel_id=1, source_target_pairs={{0,4},{16,20},{2,6},{18,22},{4,0},{20,16},{6,2},{22,18},{8,12},{24... | collective-permute-start | bytes 688136 | tf_op jit(solution)/shard_map/ppermute | solution.py:35
  157.9 5.8 %collective-permute-start.19 = (bf16[56,2048]{1,0:T(8,128)(2,1)S(1)}, bf16[56,2048]{1,0:T(8,128)(2,1)S(1)}, u32[]{:S(2)}, u32[]{:S(2)}) collective-permute-start(bf16[56,2048]{1,0:T(8,128)(2,1)S(1)} %get-tuple-element.44), channel_id=1, source_target_pairs={{0,20},{16,4},{2,22},{18,6},{4,16},{20,0},{6,18},{22,2},{8,28},{24... | collective-permute-start | bytes 688136 | tf_op jit(solution)/shard_map/ppermute | solution.py:35
  158.5 10.6 %collective-permute-start.20 = (bf16[56,2048]{1,0:T(8,128)(2,1)S(1)}, bf16[56,2048]{1,0:T(8,128)(2,1)S(1)}, u32[]{:S(2)}, u32[]{:S(2)}) collective-permute-start(bf16[56,2048]{1,0:T(8,128)(2,1)S(1)} %get-tuple-element.45), channel_id=1, source_target_pairs={{0,6},{16,22},{2,4},{18,20},{4,2},{20,18},{6,0},{22,16},{8,14},{24... | collective-permute-start | bytes 688136 | tf_op jit(solution)/shard_map/ppermute | solution.py:35
  163.7 10.1 %collective-permute-start.21 = (bf16[56,2048]{1,0:T(8,128)(2,1)S(1)}, bf16[56,2048]{1,0:T(8,128)(2,1)S(1)}, u32[]{:S(2)}, u32[]{:S(2)}) collective-permute-start(bf16[56,2048]{1,0:T(8,128)(2,1)S(1)} %get-tuple-element.38), channel_id=1, source_target_pairs={{0,22},{16,6},{2,20},{18,4},{4,18},{20,2},{6,16},{22,0},{8,30},{24... | collective-permute-start | bytes 688136 | tf_op jit(solution)/shard_map/ppermute | solution.py:35
  169.1 8.3 %collective-permute-start.31 = (bf16[56,2048]{1,0:T(8,128)(2,1)S(1)}, bf16[56,2048]{1,0:T(8,128)(2,1)S(1)}, u32[]{:S(2)}, u32[]{:S(2)}) collective-permute-start(bf16[56,2048]{1,0:T(8,128)(2,1)S(1)} %get-tuple-element.24), channel_id=1, source_target_pairs={{0,16},{16,0},{2,18},{18,2},{4,20},{20,4},{6,22},{22,6},{8,24},{24... | collective-permute-start | bytes 688136 | tf_op jit(solution)/shard_map/ppermute | solution.py:35
  173.8 5.6 %collective-permute-start.32 = (bf16[56,2048]{1,0:T(8,128)(2,1)S(1)}, bf16[56,2048]{1,0:T(8,128)(2,1)S(1)}, u32[]{:S(2)}, u32[]{:S(2)}) collective-permute-start(bf16[56,2048]{1,0:T(8,128)(2,1)S(1)} %get-tuple-element.25), channel_id=1, source_target_pairs={{0,2},{16,18},{2,0},{18,16},{4,6},{20,22},{6,4},{22,20},{8,10},{24... | collective-permute-start | bytes 688136 | tf_op jit(solution)/shard_map/ppermute | solution.py:35
  177.4 5.9 %collective-permute-start.33 = (bf16[56,2048]{1,0:T(8,128)(2,1)S(1)}, bf16[56,2048]{1,0:T(8,128)(2,1)S(1)}, u32[]{:S(2)}, u32[]{:S(2)}) collective-permute-start(bf16[56,2048]{1,0:T(8,128)(2,1)S(1)} %get-tuple-element.26), channel_id=1, source_target_pairs={{0,18},{16,2},{2,16},{18,0},{4,22},{20,6},{6,20},{22,4},{8,26},{24... | collective-permute-start | bytes 688136 | tf_op jit(solution)/shard_map/ppermute | solution.py:35
  179.4 5.2 %collective-permute-start.34 = (bf16[56,2048]{1,0:T(8,128)(2,1)S(1)}, bf16[56,2048]{1,0:T(8,128)(2,1)S(1)}, u32[]{:S(2)}, u32[]{:S(2)}) collective-permute-start(bf16[56,2048]{1,0:T(8,128)(2,1)S(1)} %get-tuple-element.27), channel_id=1, source_target_pairs={{0,4},{16,20},{2,6},{18,22},{4,0},{20,16},{6,2},{22,18},{8,12},{24... | collective-permute-start | bytes 688136 | tf_op jit(solution)/shard_map/ppermute | solution.py:35
  183.3 6.1 %collective-permute-start.35 = (bf16[56,2048]{1,0:T(8,128)(2,1)S(1)}, bf16[56,2048]{1,0:T(8,128)(2,1)S(1)}, u32[]{:S(2)}, u32[]{:S(2)}) collective-permute-start(bf16[56,2048]{1,0:T(8,128)(2,1)S(1)} %get-tuple-element.28), channel_id=1, source_target_pairs={{0,20},{16,4},{2,22},{18,6},{4,16},{20,0},{6,18},{22,2},{8,28},{24... | collective-permute-start | bytes 688136 | tf_op jit(solution)/shard_map/ppermute | solution.py:35
  184.6 8.9 %collective-permute-start.36 = (bf16[56,2048]{1,0:T(8,128)(2,1)S(1)}, bf16[56,2048]{1,0:T(8,128)(2,1)S(1)}, u32[]{:S(2)}, u32[]{:S(2)}) collective-permute-start(bf16[56,2048]{1,0:T(8,128)(2,1)S(1)} %get-tuple-element.29), channel_id=1, source_target_pairs={{0,6},{16,22},{2,4},{18,20},{4,2},{20,18},{6,0},{22,16},{8,14},{24... | collective-permute-start | bytes 688136 | tf_op jit(solution)/shard_map/ppermute | solution.py:35
  189.4 9.1 %collective-permute-start.37 = (bf16[56,2048]{1,0:T(8,128)(2,1)S(1)}, bf16[56,2048]{1,0:T(8,128)(2,1)S(1)}, u32[]{:S(2)}, u32[]{:S(2)}) collective-permute-start(bf16[56,2048]{1,0:T(8,128)(2,1)S(1)} %get-tuple-element.22), channel_id=1, source_target_pairs={{0,22},{16,6},{2,20},{18,4},{4,18},{20,2},{6,16},{22,0},{8,30},{24... | collective-permute-start | bytes 688136 | tf_op jit(solution)/shard_map/ppermute | solution.py:35
  193.5 5.9 %collective-permute-start.39 = (f32[2,128]{1,0:T(2,128)S(1)}, f32[2,128]{1,0:T(2,128)S(1)}, u32[]{:S(2)}, u32[]{:S(2)}) collective-permute-start(f32[2,128]{1,0:T(2,128)S(1)} %pad_maximum_fusion.11), channel_id=1, source_target_pairs={{0,8},{16,24},{2,10},{18,26},{4,12},{20,28},{6,14},{22,30},{8,0},{... | collective-permute-start | bytes 3080 | tf_op jit(solution)/shard_map/ppermute | solution.py:35
  198.5 29.5 %collective-permute-start.22 = (bf16[128,2048]{1,0:T(8,128)(2,1)S(1)}, bf16[128,2048]{1,0:T(8,128)(2,1)S(1)}, u32[]{:S(2)}, u32[]{:S(2)}) collective-permute-start(bf16[128,2048]{1,0:T(8,128)(2,1)S(1)} %slice.450), channel_id=1, source_target_pairs={{0,8},{16,24},{2,10},{18,26},{4,12},{20,28},{6,14},{22,30},{8,0},{... | collective-permute-start | bytes 1572872 | tf_op jit(solution)/shard_map/ppermute | solution.py:35
  199.4 49.2 %collective-permute-start.38 = (bf16[128,2048]{1,0:T(8,128)(2,1)S(1)}, bf16[128,2048]{1,0:T(8,128)(2,1)S(1)}, u32[]{:S(2)}, u32[]{:S(2)}) collective-permute-start(bf16[128,2048]{1,0:T(8,128)(2,1)S(1)} %slice.449), channel_id=1, source_target_pairs={{0,8},{16,24},{2,10},{18,26},{4,12},{20,28},{6,14},{22,30},{8,0},{... | collective-permute-start | bytes 1572872 | tf_op jit(solution)/shard_map/ppermute | solution.py:35
  229.2 29.8 %collective-permute-start.45 = (bf16[1024,768]{1,0:T(8,128)(2,1)S(1)}, bf16[1024,768]{1,0:T(8,128)(2,1)S(1)}, u32[]{:S(2)}, u32[]{:S(2)}) collective-permute-start(bf16[1024,768]{1,0:T(8,128)(2,1)S(1)} %add_convert_fusion), channel_id=1, source_target_pairs={{1,16},{3,18},{5,20},{7,22},{9,24},{11,26},{13,28},{15,30},{16,1},... | collective-permute-start | bytes 4718600 | tf_op jit(solution)/shard_map/ppermute | solution.py:44
  242.0 33.9 %collective-permute-start.43 = (bf16[1024,768]{1,0:T(8,128)(2,1)S(1)}, bf16[1024,768]{1,0:T(8,128)(2,1)S(1)}, u32[]{:S(2)}, u32[]{:S(2)}) collective-permute-start(bf16[1024,768]{1,0:T(8,128)(2,1)S(1)} %add_convert_fusion.1), channel_id=1, source_target_pairs={{1,16},{3,18},{5,20},{7,22},{9,24},{11,26},{13,28},{15,30},{16,1},... | collective-permute-start | bytes 4718600 | tf_op jit(solution)/shard_map/ppermute | solution.py:44
  245.0 47.8 %collective-permute-start.41 = (bf16[1024,768]{1,0:T(8,128)(2,1)S(1)}, bf16[1024,768]{1,0:T(8,128)(2,1)S(1)}, u32[]{:S(2)}, u32[]{:S(2)}) collective-permute-start(bf16[1024,768]{1,0:T(8,128)(2,1)S(1)} %add_convert_fusion.2), channel_id=1, source_target_pairs={{1,16},{3,18},{5,20},{7,22},{9,24},{11,26},{13,28},{15,30},{16,1},... | collective-permute-start | bytes 4718600 | tf_op jit(solution)/shard_map/ppermute | solution.py:44
  (9 other events, 59.5 us)
where the time goes:
time: 299 us; the launch traced here: 294 us
  waiting for transfers between devices  179 us (60%)
  starting transfers between devices  70.6 us (24%)
  matrix products  24 us (8%)
  other arithmetic  17.8 us (6%)
    ppermute x40, waiting for transfers between devices, move(): return lax.ppermute(value, AXES, pairs)  139 us
    ppermute x40, starting transfers between devices, move(): return lax.ppermute(value, AXES, pairs)  43.3 us
    ppermute x6, waiting for transfers between devices, transpose(): moved = lax.ppermute(value, AXES, pairs)  39.6 us
    ppermute x6, starting transfers between devices, transpose(): moved = lax.ppermute(value, AXES, pairs)  27.4 us
    dot_general x8, matrix products, dot(): return jnp.dot(left_side, right_side, preferred_element_type=jnp.float32)  8.89 us
    dot_general x8, matrix products, contract_first(): lax.dot_general(left_side, right_side, (((0,), (0,)), ((), ())), preferre...  7.81 us
    dot_general x7, matrix products, contract_last(): lax.dot_general(left_side, right_side, (((1,), (1,)), ((), ())), preferre...  7.27 us
    select_n x6, other arithmetic, transpose(): return lax.optimization_barrier(jnp.where(stays, value, moved))  7.23 us
  transfers between devices with their start and end apart: 46, of which 28 were waited for; matrix products, arithmetic and copies ran while one was open for 11% of the time, Pallas kernels for 0%

commit v1 on v0

v1 whole, which is shorter than its diff:
```python
import jax
import jax.numpy as jnp
import numpy as np
from jax import lax
from jax.sharding import PartitionSpec as P


TOPK = 2
AXES = ("dp", "expert")


def contract_last(left_side, right_side):
    return lax.dot_general(
        left_side, right_side, (((1,), (1,)), ((), ())), preferred_element_type=jnp.float32
    )


def contract_first(left_side, right_side):
    return lax.dot_general(
        left_side, right_side, (((0,), (0,)), ((), ())), preferred_element_type=jnp.float32
    )


def dot(left_side, right_side):
    return jnp.dot(left_side, right_side, preferred_element_type=jnp.float32)


def make_body(n_dp, n_ex):
    def physical(v, e):
        return ((v >> 1) * 2 + (e & 1)) * n_ex + (e >> 1) * 2 + (v & 1)

    def move(value, where):
        pairs = [
            (physical(v, e), physical(*where(v, e))) for v in range(n_dp) for e in range(n_ex)
        ]
        return lax.ppermute(value, AXES, pairs)

    def transpose(value):
        pairs = [
            (i * n_ex + c, ((i & ~1) | (c & 1)) * n_ex + ((c & ~1) | (i & 1)))
            for i in range(n_dp)
            for c in range(n_ex)
            if (i & 1) != (c & 1)
        ]
        moved = lax.ppermute(value, AXES, pairs)
        stays = (lax.axis_index("dp") & 1) == (lax.axis_index("expert") & 1)
        return lax.optimization_barrier(jnp.where(stays, value, moved))

    half = n_ex // 2

    def across(value, mask):
        return move(value, lambda v, e: (v, e ^ mask))

    def to_owner(value, d):
        return move(value, lambda v, e: (v, e ^ d))

    def to_part(value, s):
        return move(value, lambda v, e: (v ^ s, e))

    def body(
        tokens, gate_weights, expert_ids, hot_experts, gate_proj, up_proj, down_proj, out_grad
    ):
        token_count, model_width = tokens.shape
        width = model_width // n_dp
        assign_count = token_count * TOPK
        cap_rows = 5 * assign_count // (4 * n_ex)
        slot_count = cap_rows + assign_count // (2 * n_ex)
        i_index = lax.axis_index("dp")
        c_index = lax.axis_index("expert")
        v_index = (i_index >> 1) * 2 + (c_index & 1)
        e_index = (c_index >> 1) * 2 + (i_index & 1)

        def turned(value):
            blocks = [value[:, s * width : (s + 1) * width] for s in range(n_dp)]
            result = []
            for s in range(n_dp):
                pick = blocks[s]
                for j in range(n_dp):
                    if j != s:
                        pick = jnp.where(v_index == (j ^ s), blocks[j], pick)
                result.append(pick)
            return result

        own_routes = jnp.concatenate([expert_ids.T.astype(jnp.float32), gate_weights.T], axis=0)
        tok_routes = across(own_routes, half)
        og_routes = across(own_routes, 1)
        tok_far = across(tokens, half)
        og_far = across(out_grad, 1)
        tok_own, tok_far = turned(tokens), turned(tok_far)
        og_own, og_far = turned(out_grad), turned(og_far)

        def gathered(shard):
            own = transpose(shard[0])
            return [own] + [to_part(own, s) for s in range(1, n_dp)]

        gate_parts = gathered(gate_proj)
        up_parts = gathered(up_proj)
        down_parts = gathered(down_proj)

        def slots(ids):
            flat_ids = ids.reshape(ids.shape[0], -1)
            order = (
                jnp.arange(token_count, dtype=jnp.int32)[None, :] * TOPK
                + jnp.arange(TOPK, dtype=jnp.int32)[:, None]
            ).reshape(-1)
            same = (flat_ids[:, :, None] == flat_ids[:, None, :]) & (
                order[:, None] < order[None, :]
            )
            slot_pos = jnp.sum(same.astype(jnp.int32), axis=1)
            hot_row = jnp.any(flat_ids[:, None, :] == hot_experts[None, :, None], axis=1)
            kept_mask = slot_pos < jnp.where(hot_row, slot_count, cap_rows)
            return jnp.where(kept_mask, flat_ids * slot_count + slot_pos, -1).reshape(ids.shape)

        routes = jnp.stack([own_routes, tok_routes, og_routes])
        codes = slots(routes[:, :TOPK].astype(jnp.int32))

        def pairing(mask):
            steps = [d for d in range(n_ex) if not d & mask]
            row_d = np.repeat(np.array(steps, np.int32), 2 * slot_count)
            row_block = np.tile(np.repeat(np.arange(2, dtype=np.int32), slot_count), len(steps))
            row_slot = np.tile(np.arange(slot_count, dtype=np.int32), 2 * len(steps))
            code = (e_index ^ jnp.asarray(row_d)) * slot_count + jnp.asarray(row_slot)
            return steps, [jnp.where(jnp.asarray(row_block) == j, code, -2) for j in range(2)]

        def hits_of(row_code, code):
            return [row_code[:, None] == code[k][None, :] for k in range(TOPK)]

        def place_of(row_code, code):
            hits = hits_of(row_code, code)
            return (hits[0] | hits[1]).astype(jnp.bfloat16)

        def scaled_of(row_code, code, weights):
            hits = hits_of(row_code, code)
            return jnp.where(
                hits[0], weights[0][None, :], jnp.where(hits[1], weights[1][None, :], 0.0)
            )

        tok_steps, tok_rows_of = pairing(half)
        og_steps, og_rows_of = pairing(1)
        tok_codes = [codes[0], codes[1]]
        og_codes = [codes[0], codes[2]]
        tok_place = [place_of(tok_rows_of[j], tok_codes[j]) for j in range(2)]
        og_place = [place_of(og_rows_of[j], og_codes[j]) for j in range(2)]
        scaled = [scaled_of(og_rows_of[j], og_codes[j], routes[2 * j, TOPK:]) for j in range(2)]
        row_weight = jnp.sum(scaled[0] + scaled[1], axis=1, keepdims=True)
        weighted = [part.astype(jnp.bfloat16) for part in scaled]
        tok_place, og_place, weighted, row_weight = lax.optimization_barrier(
            (tok_place, og_place, weighted, row_weight)
        )
        swap = np.array([q // 2 + (q % 2) * half for q in range(n_ex)])
        old_row = (swap[:, None] * slot_count + np.arange(slot_count)[None, :]).reshape(-1)
        row_range = jnp.arange(n_ex * slot_count, dtype=jnp.int32)
        reorder = lax.optimization_barrier(
            (jnp.asarray(old_row, jnp.int32)[:, None] == row_range[None, :]).astype(jnp.bfloat16)
        )

        chunk = 2 * slot_count

        def exchange(rows, steps):
            pieces = [rows[j * chunk : (j + 1) * chunk] for j in range(half)]
            moved = [to_owner(pieces[j], steps[j]) for j in range(1, half)]
            return jnp.concatenate([pieces[0]] + moved, axis=0)

        tok_first = [dot(tok_place[0], part) for part in tok_own]
        og_first = [dot(og_place[0], part) for part in og_own]
        tok_rows = jnp.concatenate(
            [
                (tok_first[s] + dot(tok_place[1], tok_far[s])).astype(jnp.bfloat16)
                for s in range(n_dp)
            ],
            axis=1,
        )
        og_rows = jnp.concatenate(
            [
                (row_weight * (og_first[s] + dot(og_place[1], og_far[s]))).astype(jnp.bfloat16)
                for s in range(n_dp)
            ],
            axis=1,
        )
        expert_rows = exchange(tok_rows, tok_steps)
        grad_in = exchange(og_rows, og_steps)
        grad_in = dot(reorder, grad_in).astype(jnp.bfloat16)

        def cols(value, s):
            return value[:, s * width : (s + 1) * width]

        def through(value, parts):
            total = dot(cols(value, 0), parts[0])
            for s in range(1, n_dp):
                total = total + dot(cols(value, s), parts[s])
            return total

        gate_act = through(expert_rows, gate_parts)
        up_act = through(expert_rows, up_parts)
        hidden = (gate_act * jax.nn.sigmoid(gate_act) * up_act).astype(jnp.bfloat16)
        gate_act, up_act, hidden = lax.optimization_barrier((gate_act, up_act, hidden))
        output = jnp.concatenate(
            [contract_last(hidden, part).astype(jnp.bfloat16) for part in down_parts], axis=1
        )
        sigmoid_act = jax.nn.sigmoid(gate_act)
        silu_act = gate_act * sigmoid_act
        output = contract_first(reorder, output).astype(jnp.bfloat16)
        returned = exchange(output, og_steps)

        grad_hidden = through(grad_in, down_parts)
        grad_up = (grad_hidden * silu_act).astype(jnp.bfloat16)
        grad_gate = (
            grad_hidden * up_act * sigmoid_act * (1.0 + gate_act * (1.0 - sigmoid_act))
        ).astype(jnp.bfloat16)
        grad_rows = jnp.concatenate(
            [
                (
                    contract_last(grad_gate, gate_parts[s])
                    + contract_last(grad_up, up_parts[s])
                ).astype(jnp.bfloat16)
                for s in range(n_dp)
            ],
            axis=1,
        )
        grad_back = exchange(grad_rows, tok_steps)

        def weight_grad(left_side, right_side):
            terms = [
                contract_first(cols(left_side, s), right_side).astype(jnp.bfloat16)
                for s in range(1, n_dp)
            ]
            terms = [to_part(terms[s - 1], s) for s in range(1, n_dp)]
            total = contract_first(cols(left_side, 0), right_side)
            for term in terms:
                total = total + term.astype(jnp.float32)
            return transpose(total.astype(jnp.bfloat16))[None]

        down_proj_grad = weight_grad(grad_in, hidden)
        gate_proj_grad = weight_grad(expert_rows, grad_gate)
        up_proj_grad = weight_grad(expert_rows, grad_up)

        def join(sides, right_side, mask):
            other = contract_first(sides[1], right_side).astype(jnp.bfloat16)
            other = across(other, mask)
            own = contract_first(sides[0], right_side)
            total = (own + other.astype(jnp.float32)).astype(jnp.bfloat16)
            return jnp.concatenate(turned(total), axis=1)

        layer_out = join(weighted, returned, 1)
        tokens_grad = join(tok_place, grad_back, half)
        late_codes, late_rows, _ = lax.optimization_barrier((og_codes, og_rows_of, returned))

        def inner_sums(og_parts, j):
            inner = contract_last(cols(returned, 0), og_parts[0])
            for s in range(1, n_dp):
                inner = inner + contract_last(cols(returned, s), og_parts[s])
            hits = hits_of(late_rows[j], late_codes[j])
            return jnp.stack([jnp.sum(jnp.where(hit, inner, 0.0), axis=0) for hit in hits])

        routing_far = inner_sums(og_far, 1)
        routing_far = across(routing_far, 1)
        routing_grad = (inner_sums(og_own, 0) + routing_far).T
        return (layer_out, tokens_grad, routing_grad, gate_proj_grad, up_proj_grad, down_proj_grad)

    return body


def solution(mesh):
    in_specs = (
        P(("dp", "expert"), None),
        P(("dp", "expert"), None),
        P(("dp", "expert"), None),
        P(),
        P("expert", "dp", None),
        P("expert", "dp", None),
        P("expert", "dp", None),
        P(("dp", "expert"), None),
    )
    out_specs = (
        P(("dp", "expert"), None),
        P(("dp", "expert"), None),
        P(("dp", "expert"), None),
        P("expert", "dp", None),
        P("expert", "dp", None),
        P("expert", "dp", None),
    )
    body = make_body(mesh.shape["dp"], mesh.shape["expert"])
    return jax.shard_map(body, mesh=mesh, in_specs=in_specs, out_specs=out_specs, check_vma=False)
```

time: 299 us -> 342 us (1.14)
  waiting for transfers between devices: 179 us -> 215 us
  starting transfers between devices: 70.6 us -> 81.2 us
  other arithmetic: 17.8 us -> 13.8 us
  matrix products: 24 us -> 27.6 us
    ppermute x40 -> x41, waiting for transfers between devices: 139 us -> 175 us  [move(): return lax.ppermute(value, AXES, pairs)]
    ppermute x40 -> x41, starting transfers between devices: 43.3 us -> 49.5 us  [move(): return lax.ppermute(value, AXES, pairs)]
    ppermute x6, starting transfers between devices: 27.4 us -> 31.7 us  [transpose(): moved = lax.ppermute(value, AXES, pairs)]
    dot_general x8 -> x15, matrix products: 8.89 us -> 10.7 us  [dot(): return jnp.dot(left_side, right_side, preferred_element_type=jnp.float32)]
    dot_general x8 -> x11, matrix products: 7.81 us -> 9.51 us  [contract_first(): lax.dot_general(left_side, right_side, (((0,), (0,)), ((), ())), preferre...]
    dot_general x7 -> x10, matrix products: 7.27 us -> 7.35 us  [contract_last(): lax.dot_general(left_side, right_side, (((1,), (1,)), ((), ())), preferre...]
  transfers between devices with their start and end apart: 46 -> 47, of which waited for: 28 -> 28; matrix products, arithmetic and copies ran while one was open for 11% -> 9% of each run, Pallas kernels for 0% -> 0%
where the time goes in v1:
time: 342 us; the launch traced here: 340 us
  waiting for transfers between devices  215 us (63%)
  starting transfers between devices  81.2 us (24%)
  matrix products  27.6 us (8%)
  other arithmetic  13.8 us (4%)
    ppermute x41, waiting for transfers between devices, move(): return lax.ppermute(value, AXES, pairs)  175 us
    ppermute x41, starting transfers between devices, move(): return lax.ppermute(value, AXES, pairs)  49.5 us
    ppermute x6, waiting for transfers between devices, transpose(): moved = lax.ppermute(value, AXES, pairs)  39.2 us
    ppermute x6, starting transfers between devices, transpose(): moved = lax.ppermute(value, AXES, pairs)  31.7 us
    dot_general x15, matrix products, dot(): return jnp.dot(left_side, right_side, preferred_element_type=jnp.float32)  10.7 us
    dot_general x11, matrix products, contract_first(): lax.dot_general(left_side, right_side, (((0,), (0,)), ((), ())), preferre...  9.51 us
    dot_general x10, matrix products, contract_last(): lax.dot_general(left_side, right_side, (((1,), (1,)), ((), ())), preferre...  7.35 us
  transfers between devices with their start and end apart: 47, of which 28 were waited for; matrix products, arithmetic and copies ran while one was open for 9% of the time, Pallas kernels for 0%

profile of v1, /device:TPU:13, one launch (start us, length us, event | category | flops | bytes accessed | tf_op | source)
XLA Modules:
  0.0 339.7 jit_solution(5801857372217016763)
XLA Ops:
  2.0 2.3 collective-permute-start
  5.8 4.8 %collective-permute-start.14 = (bf16[1024,768]{1,0:T(8,128)(2,1)}, bf16[1024,768]{1,0:T(8,128)(2,1)S(1)}, u32[]{:S(2)}, u32[]{:S(2)}) collective-permute-start(bf16[1024,768]{1,0:T(8,128)(2,1)} %bitcast.106), channel_id=1, source_target_pairs={{1,16},{3,18},{5,20},{7,22},{9,24},{11,26},{13,28},{15,30},{16,1},... | collective-permute-start | bytes 4718600 | tf_op jit(solution)/shard_map/ppermute | solution.py:45
  10.8 1.6 fusion.5
  13.2 1.9 collective-permute-start.12
  15.1 3.6 %collective-permute-start.10 = (bf16[1024,768]{1,0:T(8,128)(2,1)}, bf16[1024,768]{1,0:T(8,128)(2,1)S(1)}, u32[]{:S(2)}, u32[]{:S(2)}) collective-permute-start(bf16[1024,768]{1,0:T(8,128)(2,1)} %bitcast.107), channel_id=1, source_target_pairs={{1,16},{3,18},{5,20},{7,22},{9,24},{11,26},{13,28},{15,30},{16,1},... | collective-permute-start | bytes 4718600 | tf_op jit(solution)/shard_map/ppermute | solution.py:45
  20.8 1.5 fusion.79
  25.8 7.8 %collective-permute-done.2 = bf16[128,2048]{1,0:T(8,128)(2,1)S(1)} collective-permute-done((bf16[128,2048]{1,0:T(8,128)(2,1)}, bf16[128,2048]{1,0:T(8,128)(2,1)S(1)}, u32[]{:S(2)}, u32[]{:S(2)}) %collective-permute-start.2) | collective-permute-done | bytes 524320 | tf_op jit(solution)/shard_map/ppermute | solution.py:36
  34.8 10.2 %collective-permute-done.25 = bf16[56,2048]{1,0:T(8,128)(2,1)S(1)} collective-permute-done((bf16[56,2048]{1,0:T(8,128)(2,1)S(1)}, bf16[56,2048]{1,0:T(8,128)(2,1)S(1)}, u32[]{:S(2)}, u32[]{:S(2)}) %collective-permute-start.25) | collective-permute-done | bytes 229408 | tf_op jit(solution)/shard_map/ppermute | solution.py:36
  44.9 6.4 %collective-permute-done.26 = bf16[56,2048]{1,0:T(8,128)(2,1)S(1)} collective-permute-done((bf16[56,2048]{1,0:T(8,128)(2,1)S(1)}, bf16[56,2048]{1,0:T(8,128)(2,1)S(1)}, u32[]{:S(2)}, u32[]{:S(2)}) %collective-permute-start.26) | collective-permute-done | bytes 229408 | tf_op jit(solution)/shard_map/ppermute | solution.py:36
  51.7 6.1 %collective-permute-done.27 = bf16[56,2048]{1,0:T(8,128)(2,1)S(1)} collective-permute-done((bf16[56,2048]{1,0:T(8,128)(2,1)S(1)}, bf16[56,2048]{1,0:T(8,128)(2,1)S(1)}, u32[]{:S(2)}, u32[]{:S(2)}) %collective-permute-start.27) | collective-permute-done | bytes 229408 | tf_op jit(solution)/shard_map/ppermute | solution.py:36
  59.1 9.6 %collective-permute-done.28 = bf16[56,2048]{1,0:T(8,128)(2,1)S(1)} collective-permute-done((bf16[56,2048]{1,0:T(8,128)(2,1)S(1)}, bf16[56,2048]{1,0:T(8,128)(2,1)S(1)}, u32[]{:S(2)}, u32[]{:S(2)}) %collective-permute-start.28) | collective-permute-done | bytes 229408 | tf_op jit(solution)/shard_map/ppermute | solution.py:36
  68.7 3.7 %collective-permute-start.29 = (bf16[56,2048]{1,0:T(8,128)(2,1)S(1)}, bf16[56,2048]{1,0:T(8,128)(2,1)S(1)}, u32[]{:S(2)}, u32[]{:S(2)}) collective-permute-start(bf16[56,2048]{1,0:T(8,128)(2,1)S(1)} %get-tuple-element.54), channel_id=1, source_target_pairs={{0,10},{16,26},{2,8},{18,24},{4,14},{20,30},{6,12},{22,28},{8,2},{... | collective-permute-start | bytes 688136 | tf_op jit(solution)/shard_map/ppermute | solution.py:36
  72.5 8.6 %collective-permute-done.29 = bf16[56,2048]{1,0:T(8,128)(2,1)S(1)} collective-permute-done((bf16[56,2048]{1,0:T(8,128)(2,1)S(1)}, bf16[56,2048]{1,0:T(8,128)(2,1)S(1)}, u32[]{:S(2)}, u32[]{:S(2)}) %collective-permute-start.29) | collective-permute-done | bytes 229408 | tf_op jit(solution)/shard_map/ppermute | solution.py:36
  82.1 9.2 %collective-permute-done.30 = bf16[56,2048]{1,0:T(8,128)(2,1)S(1)} collective-permute-done((bf16[56,2048]{1,0:T(8,128)(2,1)S(1)}, bf16[56,2048]{1,0:T(8,128)(2,1)S(1)}, u32[]{:S(2)}, u32[]{:S(2)}) %collective-permute-start.30) | collective-permute-done | bytes 229408 | tf_op jit(solution)/shard_map/ppermute | solution.py:36
  91.3 2.1 collective-permute-start.9
  94.7 10.5 %collective-permute-done.3 = bf16[56,2048]{1,0:T(8,128)(2,1)S(1)} collective-permute-done((bf16[56,2048]{1,0:T(8,128)(2,1)S(1)}, bf16[56,2048]{1,0:T(8,128)(2,1)S(1)}, u32[]{:S(2)}, u32[]{:S(2)}) %collective-permute-start.3) | collective-permute-done | bytes 229408 | tf_op jit(solution)/shard_map/ppermute | solution.py:36
  105.3 6.4 %collective-permute-done.4 = bf16[56,2048]{1,0:T(8,128)(2,1)S(1)} collective-permute-done((bf16[56,2048]{1,0:T(8,128)(2,1)S(1)}, bf16[56,2048]{1,0:T(8,128)(2,1)S(1)}, u32[]{:S(2)}, u32[]{:S(2)}) %collective-permute-start.4) | collective-permute-done | bytes 229408 | tf_op jit(solution)/shard_map/ppermute | solution.py:36
  111.7 6.6 %collective-permute-done.5 = bf16[56,2048]{1,0:T(8,128)(2,1)S(1)} collective-permute-done((bf16[56,2048]{1,0:T(8,128)(2,1)S(1)}, bf16[56,2048]{1,0:T(8,128)(2,1)S(1)}, u32[]{:S(2)}, u32[]{:S(2)}) %collective-permute-start.5) | collective-permute-done | bytes 229408 | tf_op jit(solution)/shard_map/ppermute | solution.py:36
  118.3 4.8 %collective-permute-done.6 = bf16[56,2048]{1,0:T(8,128)(2,1)S(1)} collective-permute-done((bf16[56,2048]{1,0:T(8,128)(2,1)S(1)}, bf16[56,2048]{1,0:T(8,128)(2,1)S(1)}, u32[]{:S(2)}, u32[]{:S(2)}) %collective-permute-start.6) | collective-permute-done | bytes 229408 | tf_op jit(solution)/shard_map/ppermute | solution.py:36
  123.2 1.9 collective-permute-start.7
  125.4 4.9 %collective-permute-start.15 = (bf16[1024,768]{1,0:T(8,128)(2,1)S(1)}, bf16[1024,768]{1,0:T(8,128)(2,1)S(1)}, u32[]{:S(2)}, u32[]{:S(2)}) collective-permute-start(bf16[1024,768]{1,0:T(8,128)(2,1)S(1)} %broadcast_select_fusion.3), channel_id=1, source_target_pairs={{0,1},{16,17},{2,3},{18,19},{4,5},{20,21},{6,7},{22,23},{8,9},{24,... | collective-permute-start | bytes 4718600 | tf_op jit(solution)/shard_map/ppermute | solution.py:36
  130.5 4.1 %collective-permute-start.11 = (bf16[1024,768]{1,0:T(8,128)(2,1)S(1)}, bf16[1024,768]{1,0:T(8,128)(2,1)S(1)}, u32[]{:S(2)}, u32[]{:S(2)}) collective-permute-start(bf16[1024,768]{1,0:T(8,128)(2,1)S(1)} %broadcast_select_fusion.5), channel_id=1, source_target_pairs={{0,1},{16,17},{2,3},{18,19},{4,5},{20,21},{6,7},{22,23},{8,9},{24,... | collective-permute-start | bytes 4718600 | tf_op jit(solution)/shard_map/ppermute | solution.py:36
  136.2 2.4 collective-permute-start.13
  153.5 2.3 collective-permute-start.38
  159.1 8.7 %collective-permute-done.32 = bf16[56,2048]{1,0:T(8,128)(2,1)S(1)} collective-permute-done((bf16[56,2048]{1,0:T(8,128)(2,1)S(1)}, bf16[56,2048]{1,0:T(8,128)(2,1)S(1)}, u32[]{:S(2)}, u32[]{:S(2)}) %collective-permute-start.32) | collective-permute-done | bytes 229408 | tf_op jit(solution)/shard_map/ppermute | solution.py:36
  168.1 6.4 %collective-permute-done.33 = bf16[56,2048]{1,0:T(8,128)(2,1)S(1)} collective-permute-done((bf16[56,2048]{1,0:T(8,128)(2,1)S(1)}, bf16[56,2048]{1,0:T(8,128)(2,1)S(1)}, u32[]{:S(2)}, u32[]{:S(2)}) %collective-permute-start.33) | collective-permute-done | bytes 229408 | tf_op jit(solution)/shard_map/ppermute | solution.py:36
  174.7 6.4 %collective-permute-done.34 = bf16[56,2048]{1,0:T(8,128)(2,1)S(1)} collective-permute-done((bf16[56,2048]{1,0:T(8,128)(2,1)S(1)}, bf16[56,2048]{1,0:T(8,128)(2,1)S(1)}, u32[]{:S(2)}, u32[]{:S(2)}) %collective-permute-start.34) | collective-permute-done | bytes 229408 | tf_op jit(solution)/shard_map/ppermute | solution.py:36
  181.2 4.8 %collective-permute-done.35 = bf16[56,2048]{1,0:T(8,128)(2,1)S(1)} collective-permute-done((bf16[56,2048]{1,0:T(8,128)(2,1)S(1)}, bf16[56,2048]{1,0:T(8,128)(2,1)S(1)}, u32[]{:S(2)}, u32[]{:S(2)}) %collective-permute-start.35) | collective-permute-done | bytes 229408 | tf_op jit(solution)/shard_map/ppermute | solution.py:36
  186.1 1.3 collective-permute-start.36
  187.4 4.4 %collective-permute-done.36 = bf16[56,2048]{1,0:T(8,128)(2,1)S(1)} collective-permute-done((bf16[56,2048]{1,0:T(8,128)(2,1)S(1)}, bf16[56,2048]{1,0:T(8,128)(2,1)S(1)}, u32[]{:S(2)}, u32[]{:S(2)}) %collective-permute-start.36) | collective-permute-done | bytes 229408 | tf_op jit(solution)/shard_map/ppermute | solution.py:36
  192.7 4.9 %collective-permute-done.37 = bf16[56,2048]{1,0:T(8,128)(2,1)S(1)} collective-permute-done((bf16[56,2048]{1,0:T(8,128)(2,1)S(1)}, bf16[56,2048]{1,0:T(8,128)(2,1)S(1)}, u32[]{:S(2)}, u32[]{:S(2)}) %collective-permute-start.37) | collective-permute-done | bytes 229408 | tf_op jit(solution)/shard_map/ppermute | solution.py:36
  197.6 1.8 collective-permute-start.22
  200.7 7.6 %collective-permute-done.16 = bf16[56,2048]{1,0:T(8,128)(2,1)S(1)} collective-permute-done((bf16[56,2048]{1,0:T(8,128)(2,1)S(1)}, bf16[56,2048]{1,0:T(8,128)(2,1)S(1)}, u32[]{:S(2)}, u32[]{:S(2)}) %collective-permute-start.16) | collective-permute-done | bytes 229408 | tf_op jit(solution)/shard_map/ppermute | solution.py:36
  208.4 6.4 %collective-permute-done.17 = bf16[56,2048]{1,0:T(8,128)(2,1)S(1)} collective-permute-done((bf16[56,2048]{1,0:T(8,128)(2,1)S(1)}, bf16[56,2048]{1,0:T(8,128)(2,1)S(1)}, u32[]{:S(2)}, u32[]{:S(2)}) %collective-permute-start.17) | collective-permute-done | bytes 229408 | tf_op jit(solution)/shard_map/ppermute | solution.py:36
  214.8 1.4 collective-permute-start.18
  216.3 6.3 %collective-permute-done.18 = bf16[56,2048]{1,0:T(8,128)(2,1)S(1)} collective-permute-done((bf16[56,2048]{1,0:T(8,128)(2,1)S(1)}, bf16[56,2048]{1,0:T(8,128)(2,1)S(1)}, u32[]{:S(2)}, u32[]{:S(2)}) %collective-permute-start.18) | collective-permute-done | bytes 229408 | tf_op jit(solution)/shard_map/ppermute | solution.py:36
  223.2 7.7 %collective-permute-done.19 = bf16[56,2048]{1,0:T(8,128)(2,1)S(1)} collective-permute-done((bf16[56,2048]{1,0:T(8,128)(2,1)S(1)}, bf16[56,2048]{1,0:T(8,128)(2,1)S(1)}, u32[]{:S(2)}, u32[]{:S(2)}) %collective-permute-start.19) | collective-permute-done | bytes 229408 | tf_op jit(solution)/shard_map/ppermute | solution.py:36
  231.8 8.7 %collective-permute-done.20 = bf16[56,2048]{1,0:T(8,128)(2,1)S(1)} collective-permute-done((bf16[56,2048]{1,0:T(8,128)(2,1)S(1)}, bf16[56,2048]{1,0:T(8,128)(2,1)S(1)}, u32[]{:S(2)}, u32[]{:S(2)}) %collective-permute-start.20) | collective-permute-done | bytes 229408 | tf_op jit(solution)/shard_map/ppermute | solution.py:36
  240.5 4.8 %collective-permute-done.21 = bf16[56,2048]{1,0:T(8,128)(2,1)S(1)} collective-permute-done((bf16[56,2048]{1,0:T(8,128)(2,1)S(1)}, bf16[56,2048]{1,0:T(8,128)(2,1)S(1)}, u32[]{:S(2)}, u32[]{:S(2)}) %collective-permute-start.21) | collective-permute-done | bytes 229408 | tf_op jit(solution)/shard_map/ppermute | solution.py:36
  245.4 8.1 %collective-permute-start.39 = (bf16[128,2048]{1,0:T(8,128)(2,1)S(1)}, bf16[128,2048]{1,0:T(8,128)(2,1)S(1)}, u32[]{:S(2)}, u32[]{:S(2)}) collective-permute-start(bf16[128,2048]{1,0:T(8,128)(2,1)S(1)} %convolution_convert_fusion.2), channel_id=1, source_target_pairs={{0,8},{16,24},{2,10},{18,26},{4,12},{20,28},{6,14},{22,30},{8,0},{... | collective-permute-start | bytes 1572872 | tf_op jit(solution)/shard_map/ppermute | solution.py:36
  257.9 11.0 %collective-permute-done.39 = bf16[128,2048]{1,0:T(8,128)(2,1)S(1)} collective-permute-done((bf16[128,2048]{1,0:T(8,128)(2,1)S(1)}, bf16[128,2048]{1,0:T(8,128)(2,1)S(1)}, u32[]{:S(2)}, u32[]{:S(2)}) %collective-permute-start.39) | collective-permute-done | bytes 524320 | tf_op jit(solution)/shard_map/ppermute | solution.py:36
  269.4 1.3 add_convert_fusion
  270.8 15.8 %collective-permute-start.46 = (bf16[1024,768]{1,0:T(8,128)(2,1)S(1)}, bf16[1024,768]{1,0:T(8,128)(2,1)S(1)}, u32[]{:S(2)}, u32[]{:S(2)}) collective-permute-start(bf16[1024,768]{1,0:T(8,128)(2,1)S(1)} %add_convert_fusion), channel_id=1, source_target_pairs={{1,16},{3,18},{5,20},{7,22},{9,24},{11,26},{13,28},{15,30},{16,1},... | collective-permute-start | bytes 4718600 | tf_op jit(solution)/shard_map/ppermute | solution.py:45
  287.6 1.9 collective-permute-start.44
  290.6 3.6 %collective-permute-start.42 = (bf16[1024,768]{1,0:T(8,128)(2,1)S(1)}, bf16[1024,768]{1,0:T(8,128)(2,1)S(1)}, u32[]{:S(2)}, u32[]{:S(2)}) collective-permute-start(bf16[1024,768]{1,0:T(8,128)(2,1)S(1)} %add_convert_fusion.2), channel_id=1, source_target_pairs={{1,16},{3,18},{5,20},{7,22},{9,24},{11,26},{13,28},{15,30},{16,1},... | collective-permute-start | bytes 4718600 | tf_op jit(solution)/shard_map/ppermute | solution.py:45
  296.5 8.1 %collective-permute-done.46 = bf16[1024,768]{1,0:T(8,128)(2,1)S(1)} collective-permute-done((bf16[1024,768]{1,0:T(8,128)(2,1)S(1)}, bf16[1024,768]{1,0:T(8,128)(2,1)S(1)}, u32[]{:S(2)}, u32[]{:S(2)}) %collective-permute-start.46) | collective-permute-done | bytes 1572896 | tf_op jit(solution)/shard_map/ppermute | solution.py:45
  306.0 15.5 %collective-permute-done.44 = bf16[1024,768]{1,0:T(8,128)(2,1)S(1)} collective-permute-done((bf16[1024,768]{1,0:T(8,128)(2,1)S(1)}, bf16[1024,768]{1,0:T(8,128)(2,1)S(1)}, u32[]{:S(2)}, u32[]{:S(2)}) %collective-permute-start.44) | collective-permute-done | bytes 1572896 | tf_op jit(solution)/shard_map/ppermute | solution.py:45
  322.8 15.5 %collective-permute-done.42 = bf16[1024,768]{1,0:T(8,128)(2,1)S(1)} collective-permute-done((bf16[1024,768]{1,0:T(8,128)(2,1)S(1)}, bf16[1024,768]{1,0:T(8,128)(2,1)S(1)}, u32[]{:S(2)}, u32[]{:S(2)}) %collective-permute-start.42) | collective-permute-done | bytes 1572896 | tf_op jit(solution)/shard_map/ppermute | solution.py:45
  (162 shorter events, 52.1 us)
Async XLA Ops:
  2.0 13.1 %collective-permute-start = (f32[4,128]{1,0:T(4,128)S(1)}, f32[4,128]{1,0:T(4,128)S(1)}, u32[]{:S(2)}, u32[]{:S(2)}) collective-permute-start(f32[4,128]{1,0:T(4,128)S(1)} %get-tuple-element.95), channel_id=1, source_target_pairs={{0,8},{16,24},{2,10},{18,26},{4,12},{20,28},{6,14},{22,30},{8,0},{... | collective-permute-start | bytes 6152 | tf_op jit(solution)/shard_map/ppermute | solution.py:36
  4.3 8.9 %collective-permute-start.1 = (f32[4,128]{1,0:T(4,128)S(1)}, f32[4,128]{1,0:T(4,128)S(1)}, u32[]{:S(2)}, u32[]{:S(2)}) collective-permute-start(f32[4,128]{1,0:T(4,128)S(1)} %get-tuple-element.95), channel_id=1, source_target_pairs={{0,16},{16,0},{2,18},{18,2},{4,20},{20,4},{6,22},{22,6},{8,24},{24... | collective-permute-start | bytes 6152 | tf_op jit(solution)/shard_map/ppermute | solution.py:36
  5.5 28.1 %collective-permute-start.2 = (bf16[128,2048]{1,0:T(8,128)(2,1)}, bf16[128,2048]{1,0:T(8,128)(2,1)S(1)}, u32[]{:S(2)}, u32[]{:S(2)}) collective-permute-start(bf16[128,2048]{1,0:T(8,128)(2,1)} %param.15), channel_id=1, source_target_pairs={{0,8},{16,24},{2,10},{18,26},{4,12},{20,28},{6,14},{22,30},{8,0},{... | collective-permute-start | bytes 1572872 | tf_op jit(solution)/shard_map/ppermute | solution.py:36
  5.6 17.9 %collective-permute-start.24 = (bf16[128,2048]{1,0:T(8,128)(2,1)}, bf16[128,2048]{1,0:T(8,128)(2,1)S(1)}, u32[]{:S(2)}, u32[]{:S(2)}) collective-permute-start(bf16[128,2048]{1,0:T(8,128)(2,1)} %param.22), channel_id=1, source_target_pairs={{0,16},{16,0},{2,18},{18,2},{4,20},{20,4},{6,22},{22,6},{8,24},{24... | collective-permute-start | bytes 1572872 | tf_op jit(solution)/shard_map/ppermute | solution.py:36
  5.8 119.2 %collective-permute-start.14 = (bf16[1024,768]{1,0:T(8,128)(2,1)}, bf16[1024,768]{1,0:T(8,128)(2,1)S(1)}, u32[]{:S(2)}, u32[]{:S(2)}) collective-permute-start(bf16[1024,768]{1,0:T(8,128)(2,1)} %bitcast.106), channel_id=1, source_target_pairs={{1,16},{3,18},{5,20},{7,22},{9,24},{11,26},{13,28},{15,30},{16,1},... | collective-permute-start | bytes 4718600 | tf_op jit(solution)/shard_map/ppermute | solution.py:45
  13.2 122.6 %collective-permute-start.12 = (bf16[1024,768]{1,0:T(8,128)(2,1)}, bf16[1024,768]{1,0:T(8,128)(2,1)S(1)}, u32[]{:S(2)}, u32[]{:S(2)}) collective-permute-start(bf16[1024,768]{1,0:T(8,128)(2,1)} %bitcast.108), channel_id=1, source_target_pairs={{1,16},{3,18},{5,20},{7,22},{9,24},{11,26},{13,28},{15,30},{16,1},... | collective-permute-start | bytes 4718600 | tf_op jit(solution)/shard_map/ppermute | solution.py:45
  15.1 110.2 %collective-permute-start.10 = (bf16[1024,768]{1,0:T(8,128)(2,1)}, bf16[1024,768]{1,0:T(8,128)(2,1)S(1)}, u32[]{:S(2)}, u32[]{:S(2)}) collective-permute-start(bf16[1024,768]{1,0:T(8,128)(2,1)} %bitcast.107), channel_id=1, source_target_pairs={{1,16},{3,18},{5,20},{7,22},{9,24},{11,26},{13,28},{15,30},{16,1},... | collective-permute-start | bytes 4718600 | tf_op jit(solution)/shard_map/ppermute | solution.py:45
  24.5 69.0 %collective-permute-start.31 = (bf16[56,2048]{1,0:T(8,128)(2,1)S(1)}, bf16[56,2048]{1,0:T(8,128)(2,1)S(1)}, u32[]{:S(2)}, u32[]{:S(2)}) collective-permute-start(bf16[56,2048]{1,0:T(8,128)(2,1)S(1)} %get-tuple-element.48), channel_id=1, source_target_pairs={{0,14},{16,30},{2,12},{18,28},{4,10},{20,26},{6,8},{22,24},{8,6},{... | collective-permute-start | bytes 688136 | tf_op jit(solution)/shard_map/ppermute | solution.py:36
  33.6 11.3 %collective-permute-start.25 = (bf16[56,2048]{1,0:T(8,128)(2,1)S(1)}, bf16[56,2048]{1,0:T(8,128)(2,1)S(1)}, u32[]{:S(2)}, u32[]{:S(2)}) collective-permute-start(bf16[56,2048]{1,0:T(8,128)(2,1)S(1)} %get-tuple-element.50), channel_id=1, source_target_pairs={{0,2},{16,18},{2,0},{18,16},{4,6},{20,22},{6,4},{22,20},{8,10},{24... | collective-permute-start | bytes 688136 | tf_op jit(solution)/shard_map/ppermute | solution.py:36
  44.9 6.4 %collective-permute-start.26 = (bf16[56,2048]{1,0:T(8,128)(2,1)S(1)}, bf16[56,2048]{1,0:T(8,128)(2,1)S(1)}, u32[]{:S(2)}, u32[]{:S(2)}) collective-permute-start(bf16[56,2048]{1,0:T(8,128)(2,1)S(1)} %get-tuple-element.51), channel_id=1, source_target_pairs={{0,4},{16,20},{2,6},{18,22},{4,0},{20,16},{6,2},{22,18},{8,12},{24... | collective-permute-start | bytes 688136 | tf_op jit(solution)/shard_map/ppermute | solution.py:36
  51.4 6.5 %collective-permute-start.27 = (bf16[56,2048]{1,0:T(8,128)(2,1)S(1)}, bf16[56,2048]{1,0:T(8,128)(2,1)S(1)}, u32[]{:S(2)}, u32[]{:S(2)}) collective-permute-start(bf16[56,2048]{1,0:T(8,128)(2,1)S(1)} %get-tuple-element.52), channel_id=1, source_target_pairs={{0,6},{16,22},{2,4},{18,20},{4,2},{20,18},{6,0},{22,16},{8,14},{24... | collective-permute-start | bytes 688136 | tf_op jit(solution)/shard_map/ppermute | solution.py:36
  57.8 10.9 %collective-permute-start.28 = (bf16[56,2048]{1,0:T(8,128)(2,1)S(1)}, bf16[56,2048]{1,0:T(8,128)(2,1)S(1)}, u32[]{:S(2)}, u32[]{:S(2)}) collective-permute-start(bf16[56,2048]{1,0:T(8,128)(2,1)S(1)} %get-tuple-element.53), channel_id=1, source_target_pairs={{0,8},{16,24},{2,10},{18,26},{4,12},{20,28},{6,14},{22,30},{8,0},{... | collective-permute-start | bytes 688136 | tf_op jit(solution)/shard_map/ppermute | solution.py:36
  68.7 56.4 %copy-start = (bf16[1,1024,768]{2,1,0:T(8,128)(2,1)S(1)}, bf16[1,1024,768]{2,1,0:T(8,128)(2,1)}, u32[]{:S(2)}) copy-start(bf16[1,1024,768]{2,1,0:T(8,128)(2,1)} %param.21) | copy-start | bytes 4718596
  68.7 12.3 %collective-permute-start.29 = (bf16[56,2048]{1,0:T(8,128)(2,1)S(1)}, bf16[56,2048]{1,0:T(8,128)(2,1)S(1)}, u32[]{:S(2)}, u32[]{:S(2)}) collective-permute-start(bf16[56,2048]{1,0:T(8,128)(2,1)S(1)} %get-tuple-element.54), channel_id=1, source_target_pairs={{0,10},{16,26},{2,8},{18,24},{4,14},{20,30},{6,12},{22,28},{8,2},{... | collective-permute-start | bytes 688136 | tf_op jit(solution)/shard_map/ppermute | solution.py:36
  81.1 10.3 %collective-permute-start.30 = (bf16[56,2048]{1,0:T(8,128)(2,1)S(1)}, bf16[56,2048]{1,0:T(8,128)(2,1)S(1)}, u32[]{:S(2)}, u32[]{:S(2)}) collective-permute-start(bf16[56,2048]{1,0:T(8,128)(2,1)S(1)} %get-tuple-element.55), channel_id=1, source_target_pairs={{0,12},{16,28},{2,14},{18,30},{4,8},{20,24},{6,10},{22,26},{8,4},{... | collective-permute-start | bytes 688136 | tf_op jit(solution)/shard_map/ppermute | solution.py:36
  91.3 47.2 %collective-permute-start.9 = (bf16[56,2048]{1,0:T(8,128)(2,1)S(1)}, bf16[56,2048]{1,0:T(8,128)(2,1)S(1)}, u32[]{:S(2)}, u32[]{:S(2)}) collective-permute-start(bf16[56,2048]{1,0:T(8,128)(2,1)S(1)} %get-tuple-element.64), channel_id=1, source_target_pairs={{0,22},{16,6},{2,20},{18,4},{4,18},{20,2},{6,16},{22,0},{8,30},{24... | collective-permute-start | bytes 688136 | tf_op jit(solution)/shard_map/ppermute | solution.py:36
  93.5 11.7 %collective-permute-start.3 = (bf16[56,2048]{1,0:T(8,128)(2,1)S(1)}, bf16[56,2048]{1,0:T(8,128)(2,1)S(1)}, u32[]{:S(2)}, u32[]{:S(2)}) collective-permute-start(bf16[56,2048]{1,0:T(8,128)(2,1)S(1)} %get-tuple-element.66), channel_id=1, source_target_pairs={{0,16},{16,0},{2,18},{18,2},{4,20},{20,4},{6,22},{22,6},{8,24},{24... | collective-permute-start | bytes 688136 | tf_op jit(solution)/shard_map/ppermute | solution.py:36
  105.2 6.5 %collective-permute-start.4 = (bf16[56,2048]{1,0:T(8,128)(2,1)S(1)}, bf16[56,2048]{1,0:T(8,128)(2,1)S(1)}, u32[]{:S(2)}, u32[]{:S(2)}) collective-permute-start(bf16[56,2048]{1,0:T(8,128)(2,1)S(1)} %get-tuple-element.67), channel_id=1, source_target_pairs={{0,2},{16,18},{2,0},{18,16},{4,6},{20,22},{6,4},{22,20},{8,10},{24... | collective-permute-start | bytes 688136 | tf_op jit(solution)/shard_map/ppermute | solution.py:36
  111.7 6.6 %collective-permute-start.5 = (bf16[56,2048]{1,0:T(8,128)(2,1)S(1)}, bf16[56,2048]{1,0:T(8,128)(2,1)S(1)}, u32[]{:S(2)}, u32[]{:S(2)}) collective-permute-start(bf16[56,2048]{1,0:T(8,128)(2,1)S(1)} %get-tuple-element.68), channel_id=1, source_target_pairs={{0,18},{16,2},{2,16},{18,0},{4,22},{20,6},{6,20},{22,4},{8,26},{24... | collective-permute-start | bytes 688136 | tf_op jit(solution)/shard_map/ppermute | solution.py:36
  118.3 4.9 %collective-permute-start.6 = (bf16[56,2048]{1,0:T(8,128)(2,1)S(1)}, bf16[56,2048]{1,0:T(8,128)(2,1)S(1)}, u32[]{:S(2)}, u32[]{:S(2)}) collective-permute-start(bf16[56,2048]{1,0:T(8,128)(2,1)S(1)} %get-tuple-element.69), channel_id=1, source_target_pairs={{0,4},{16,20},{2,6},{18,22},{4,0},{20,16},{6,2},{22,18},{8,12},{24... | collective-permute-start | bytes 688136 | tf_op jit(solution)/shard_map/ppermute | solution.py:36
  123.2 7.3 %collective-permute-start.7 = (bf16[56,2048]{1,0:T(8,128)(2,1)S(1)}, bf16[56,2048]{1,0:T(8,128)(2,1)S(1)}, u32[]{:S(2)}, u32[]{:S(2)}) collective-permute-start(bf16[56,2048]{1,0:T(8,128)(2,1)S(1)} %get-tuple-element.70), channel_id=1, source_target_pairs={{0,20},{16,4},{2,22},{18,6},{4,16},{20,0},{6,18},{22,2},{8,28},{24... | collective-permute-start | bytes 688136 | tf_op jit(solution)/shard_map/ppermute | solution.py:36
  125.1 9.5 %collective-permute-start.8 = (bf16[56,2048]{1,0:T(8,128)(2,1)S(1)}, bf16[56,2048]{1,0:T(8,128)(2,1)S(1)}, u32[]{:S(2)}, u32[]{:S(2)}) collective-permute-start(bf16[56,2048]{1,0:T(8,128)(2,1)S(1)} %get-tuple-element.71), channel_id=1, source_target_pairs={{0,6},{16,22},{2,4},{18,20},{4,2},{20,18},{6,0},{22,16},{8,14},{24... | collective-permute-start | bytes 688136 | tf_op jit(solution)/shard_map/ppermute | solution.py:36
  125.4 13.2 %collective-permute-start.15 = (bf16[1024,768]{1,0:T(8,128)(2,1)S(1)}, bf16[1024,768]{1,0:T(8,128)(2,1)S(1)}, u32[]{:S(2)}, u32[]{:S(2)}) collective-permute-start(bf16[1024,768]{1,0:T(8,128)(2,1)S(1)} %broadcast_select_fusion.3), channel_id=1, source_target_pairs={{0,1},{16,17},{2,3},{18,19},{4,5},{20,21},{6,7},{22,23},{8,9},{24,... | collective-permute-start | bytes 4718600 | tf_op jit(solution)/shard_map/ppermute | solution.py:36
  130.5 9.0 %collective-permute-start.11 = (bf16[1024,768]{1,0:T(8,128)(2,1)S(1)}, bf16[1024,768]{1,0:T(8,128)(2,1)S(1)}, u32[]{:S(2)}, u32[]{:S(2)}) collective-permute-start(bf16[1024,768]{1,0:T(8,128)(2,1)S(1)} %broadcast_select_fusion.5), channel_id=1, source_target_pairs={{0,1},{16,17},{2,3},{18,19},{4,5},{20,21},{6,7},{22,23},{8,9},{24,... | collective-permute-start | bytes 4718600 | tf_op jit(solution)/shard_map/ppermute | solution.py:36
  136.2 6.0 %collective-permute-start.13 = (bf16[1024,768]{1,0:T(8,128)(2,1)S(1)}, bf16[1024,768]{1,0:T(8,128)(2,1)S(1)}, u32[]{:S(2)}, u32[]{:S(2)}) collective-permute-start(bf16[1024,768]{1,0:T(8,128)(2,1)S(1)} %broadcast_select_fusion.4), channel_id=1, source_target_pairs={{0,1},{16,17},{2,3},{18,19},{4,5},{20,21},{6,7},{22,23},{8,9},{24,... | collective-permute-start | bytes 4718600 | tf_op jit(solution)/shard_map/ppermute | solution.py:36
  150.9 118.6 %collective-permute-start.45 = (bf16[1024,768]{1,0:T(8,128)(2,1)S(1)}, bf16[1024,768]{1,0:T(8,128)(2,1)S(1)}, u32[]{:S(2)}, u32[]{:S(2)}) collective-permute-start(bf16[1024,768]{1,0:T(8,128)(2,1)S(1)} %convolution_convert_fusion.4), channel_id=1, source_target_pairs={{0,1},{16,17},{2,3},{18,19},{4,5},{20,21},{6,7},{22,23},{8,9},{24,... | collective-permute-start | bytes 4718600 | tf_op jit(solution)/shard_map/ppermute | solution.py:36
  151.0 135.6 %collective-permute-start.43 = (bf16[1024,768]{1,0:T(8,128)(2,1)S(1)}, bf16[1024,768]{1,0:T(8,128)(2,1)S(1)}, u32[]{:S(2)}, u32[]{:S(2)}) collective-permute-start(bf16[1024,768]{1,0:T(8,128)(2,1)S(1)} %convolution_convert_fusion.5), channel_id=1, source_target_pairs={{0,1},{16,17},{2,3},{18,19},{4,5},{20,21},{6,7},{22,23},{8,9},{24,... | collective-permute-start | bytes 4718600 | tf_op jit(solution)/shard_map/ppermute | solution.py:36
  151.4 138.1 %collective-permute-start.41 = (bf16[1024,768]{1,0:T(8,128)(2,1)S(1)}, bf16[1024,768]{1,0:T(8,128)(2,1)S(1)}, u32[]{:S(2)}, u32[]{:S(2)}) collective-permute-start(bf16[1024,768]{1,0:T(8,128)(2,1)S(1)} %convolution_convert_fusion.6), channel_id=1, source_target_pairs={{0,1},{16,17},{2,3},{18,19},{4,5},{20,21},{6,7},{22,23},{8,9},{24,... | collective-permute-start | bytes 4718600 | tf_op jit(solution)/shard_map/ppermute | solution.py:36
  153.5 46.0 %collective-permute-start.38 = (bf16[56,2048]{1,0:T(8,128)(2,1)S(1)}, bf16[56,2048]{1,0:T(8,128)(2,1)S(1)}, u32[]{:S(2)}, u32[]{:S(2)}) collective-permute-start(bf16[56,2048]{1,0:T(8,128)(2,1)S(1)} %get-tuple-element.40), channel_id=1, source_target_pairs={{0,22},{16,6},{2,20},{18,4},{4,18},{20,2},{6,16},{22,0},{8,30},{24... | collective-permute-start | bytes 688136 | tf_op jit(solution)/shard_map/ppermute | solution.py:36
  155.8 12.0 %collective-permute-start.32 = (bf16[56,2048]{1,0:T(8,128)(2,1)S(1)}, bf16[56,2048]{1,0:T(8,128)(2,1)S(1)}, u32[]{:S(2)}, u32[]{:S(2)}) collective-permute-start(bf16[56,2048]{1,0:T(8,128)(2,1)S(1)} %get-tuple-element.42), channel_id=1, source_target_pairs={{0,16},{16,0},{2,18},{18,2},{4,20},{20,4},{6,22},{22,6},{8,24},{24... | collective-permute-start | bytes 688136 | tf_op jit(solution)/shard_map/ppermute | solution.py:36
  167.8 6.7 %collective-permute-start.33 = (bf16[56,2048]{1,0:T(8,128)(2,1)S(1)}, bf16[56,2048]{1,0:T(8,128)(2,1)S(1)}, u32[]{:S(2)}, u32[]{:S(2)}) collective-permute-start(bf16[56,2048]{1,0:T(8,128)(2,1)S(1)} %get-tuple-element.43), channel_id=1, source_target_pairs={{0,2},{16,18},{2,0},{18,16},{4,6},{20,22},{6,4},{22,20},{8,10},{24... | collective-permute-start | bytes 688136 | tf_op jit(solution)/shard_map/ppermute | solution.py:36
  174.5 6.7 %collective-permute-start.34 = (bf16[56,2048]{1,0:T(8,128)(2,1)S(1)}, bf16[56,2048]{1,0:T(8,128)(2,1)S(1)}, u32[]{:S(2)}, u32[]{:S(2)}) collective-permute-start(bf16[56,2048]{1,0:T(8,128)(2,1)S(1)} %get-tuple-element.44), channel_id=1, source_target_pairs={{0,18},{16,2},{2,16},{18,0},{4,22},{20,6},{6,20},{22,4},{8,26},{24... | collective-permute-start | bytes 688136 | tf_op jit(solution)/shard_map/ppermute | solution.py:36
  181.2 4.9 %collective-permute-start.35 = (bf16[56,2048]{1,0:T(8,128)(2,1)S(1)}, bf16[56,2048]{1,0:T(8,128)(2,1)S(1)}, u32[]{:S(2)}, u32[]{:S(2)}) collective-permute-start(bf16[56,2048]{1,0:T(8,128)(2,1)S(1)} %get-tuple-element.45), channel_id=1, source_target_pairs={{0,4},{16,20},{2,6},{18,22},{4,0},{20,16},{6,2},{22,18},{8,12},{24... | collective-permute-start | bytes 688136 | tf_op jit(solution)/shard_map/ppermute | solution.py:36
  186.1 5.8 %collective-permute-start.36 = (bf16[56,2048]{1,0:T(8,128)(2,1)S(1)}, bf16[56,2048]{1,0:T(8,128)(2,1)S(1)}, u32[]{:S(2)}, u32[]{:S(2)}) collective-permute-start(bf16[56,2048]{1,0:T(8,128)(2,1)S(1)} %get-tuple-element.46), channel_id=1, source_target_pairs={{0,20},{16,4},{2,22},{18,6},{4,16},{20,0},{6,18},{22,2},{8,28},{24... | collective-permute-start | bytes 688136 | tf_op jit(solution)/shard_map/ppermute | solution.py:36
  191.8 5.8 %collective-permute-start.37 = (bf16[56,2048]{1,0:T(8,128)(2,1)S(1)}, bf16[56,2048]{1,0:T(8,128)(2,1)S(1)}, u32[]{:S(2)}, u32[]{:S(2)}) collective-permute-start(bf16[56,2048]{1,0:T(8,128)(2,1)S(1)} %get-tuple-element.47), channel_id=1, source_target_pairs={{0,6},{16,22},{2,4},{18,20},{4,2},{20,18},{6,0},{22,16},{8,14},{24... | collective-permute-start | bytes 688136 | tf_op jit(solution)/shard_map/ppermute | solution.py:36
  197.6 55.9 %collective-permute-start.22 = (bf16[56,2048]{1,0:T(8,128)(2,1)S(1)}, bf16[56,2048]{1,0:T(8,128)(2,1)S(1)}, u32[]{:S(2)}, u32[]{:S(2)}) collective-permute-start(bf16[56,2048]{1,0:T(8,128)(2,1)S(1)} %get-tuple-element.56), channel_id=1, source_target_pairs={{0,14},{16,30},{2,12},{18,28},{4,10},{20,26},{6,8},{22,24},{8,6},{... | collective-permute-start | bytes 688136 | tf_op jit(solution)/shard_map/ppermute | solution.py:36
  199.5 8.8 %collective-permute-start.16 = (bf16[56,2048]{1,0:T(8,128)(2,1)S(1)}, bf16[56,2048]{1,0:T(8,128)(2,1)S(1)}, u32[]{:S(2)}, u32[]{:S(2)}) collective-permute-start(bf16[56,2048]{1,0:T(8,128)(2,1)S(1)} %get-tuple-element.62), channel_id=1, source_target_pairs={{0,2},{16,18},{2,0},{18,16},{4,6},{20,22},{6,4},{22,20},{8,10},{24... | collective-permute-start | bytes 688136 | tf_op jit(solution)/shard_map/ppermute | solution.py:36
  208.3 6.5 %collective-permute-start.17 = (bf16[56,2048]{1,0:T(8,128)(2,1)S(1)}, bf16[56,2048]{1,0:T(8,128)(2,1)S(1)}, u32[]{:S(2)}, u32[]{:S(2)}) collective-permute-start(bf16[56,2048]{1,0:T(8,128)(2,1)S(1)} %get-tuple-element.61), channel_id=1, source_target_pairs={{0,4},{16,20},{2,6},{18,22},{4,0},{20,16},{6,2},{22,18},{8,12},{24... | collective-permute-start | bytes 688136 | tf_op jit(solution)/shard_map/ppermute | solution.py:36
  214.8 7.7 %collective-permute-start.18 = (bf16[56,2048]{1,0:T(8,128)(2,1)S(1)}, bf16[56,2048]{1,0:T(8,128)(2,1)S(1)}, u32[]{:S(2)}, u32[]{:S(2)}) collective-permute-start(bf16[56,2048]{1,0:T(8,128)(2,1)S(1)} %get-tuple-element.60), channel_id=1, source_target_pairs={{0,6},{16,22},{2,4},{18,20},{4,2},{20,18},{6,0},{22,16},{8,14},{24... | collective-permute-start | bytes 688136 | tf_op jit(solution)/shard_map/ppermute | solution.py:36
  222.5 8.4 %collective-permute-start.19 = (bf16[56,2048]{1,0:T(8,128)(2,1)S(1)}, bf16[56,2048]{1,0:T(8,128)(2,1)S(1)}, u32[]{:S(2)}, u32[]{:S(2)}) collective-permute-start(bf16[56,2048]{1,0:T(8,128)(2,1)S(1)} %get-tuple-element.59), channel_id=1, source_target_pairs={{0,8},{16,24},{2,10},{18,26},{4,12},{20,28},{6,14},{22,30},{8,0},{... | collective-permute-start | bytes 688136 | tf_op jit(solution)/shard_map/ppermute | solution.py:36
  230.9 9.6 %collective-permute-start.20 = (bf16[56,2048]{1,0:T(8,128)(2,1)S(1)}, bf16[56,2048]{1,0:T(8,128)(2,1)S(1)}, u32[]{:S(2)}, u32[]{:S(2)}) collective-permute-start(bf16[56,2048]{1,0:T(8,128)(2,1)S(1)} %get-tuple-element.58), channel_id=1, source_target_pairs={{0,10},{16,26},{2,8},{18,24},{4,14},{20,30},{6,12},{22,28},{8,2},{... | collective-permute-start | bytes 688136 | tf_op jit(solution)/shard_map/ppermute | solution.py:36
  240.5 4.9 %collective-permute-start.21 = (bf16[56,2048]{1,0:T(8,128)(2,1)S(1)}, bf16[56,2048]{1,0:T(8,128)(2,1)S(1)}, u32[]{:S(2)}, u32[]{:S(2)}) collective-permute-start(bf16[56,2048]{1,0:T(8,128)(2,1)S(1)} %get-tuple-element.57), channel_id=1, source_target_pairs={{0,12},{16,28},{2,14},{18,30},{4,8},{20,24},{6,10},{22,26},{8,4},{... | collective-permute-start | bytes 688136 | tf_op jit(solution)/shard_map/ppermute | solution.py:36
  245.4 23.6 %collective-permute-start.39 = (bf16[128,2048]{1,0:T(8,128)(2,1)S(1)}, bf16[128,2048]{1,0:T(8,128)(2,1)S(1)}, u32[]{:S(2)}, u32[]{:S(2)}) collective-permute-start(bf16[128,2048]{1,0:T(8,128)(2,1)S(1)} %convolution_convert_fusion.2), channel_id=1, source_target_pairs={{0,8},{16,24},{2,10},{18,26},{4,12},{20,28},{6,14},{22,30},{8,0},{... | collective-permute-start | bytes 1572872 | tf_op jit(solution)/shard_map/ppermute | solution.py:36
  254.4 2.5 collective-permute-start.40
  256.9 37.4 %collective-permute-start.23 = (bf16[128,2048]{1,0:T(8,128)(2,1)S(1)}, bf16[128,2048]{1,0:T(8,128)(2,1)S(1)}, u32[]{:S(2)}, u32[]{:S(2)}) collective-permute-start(bf16[128,2048]{1,0:T(8,128)(2,1)S(1)} %convolution_convert_fusion.3), channel_id=1, source_target_pairs={{0,16},{16,0},{2,18},{18,2},{4,20},{20,4},{6,22},{22,6},{8,24},{24... | collective-permute-start | bytes 1572872 | tf_op jit(solution)/shard_map/ppermute | solution.py:36
  270.8 33.9 %collective-permute-start.46 = (bf16[1024,768]{1,0:T(8,128)(2,1)S(1)}, bf16[1024,768]{1,0:T(8,128)(2,1)S(1)}, u32[]{:S(2)}, u32[]{:S(2)}) collective-permute-start(bf16[1024,768]{1,0:T(8,128)(2,1)S(1)} %add_convert_fusion), channel_id=1, source_target_pairs={{1,16},{3,18},{5,20},{7,22},{9,24},{11,26},{13,28},{15,30},{16,1},... | collective-permute-start | bytes 4718600 | tf_op jit(solution)/shard_map/ppermute | solution.py:45
  287.6 33.9 %collective-permute-start.44 = (bf16[1024,768]{1,0:T(8,128)(2,1)S(1)}, bf16[1024,768]{1,0:T(8,128)(2,1)S(1)}, u32[]{:S(2)}, u32[]{:S(2)}) collective-permute-start(bf16[1024,768]{1,0:T(8,128)(2,1)S(1)} %add_convert_fusion.1), channel_id=1, source_target_pairs={{1,16},{3,18},{5,20},{7,22},{9,24},{11,26},{13,28},{15,30},{16,1},... | collective-permute-start | bytes 4718600 | tf_op jit(solution)/shard_map/ppermute | solution.py:45
  290.6 47.7 %collective-permute-start.42 = (bf16[1024,768]{1,0:T(8,128)(2,1)S(1)}, bf16[1024,768]{1,0:T(8,128)(2,1)S(1)}, u32[]{:S(2)}, u32[]{:S(2)}) collective-permute-start(bf16[1024,768]{1,0:T(8,128)(2,1)S(1)} %add_convert_fusion.2), channel_id=1, source_target_pairs={{1,16},{3,18},{5,20},{7,22},{9,24},{11,26},{13,28},{15,30},{16,1},... | collective-permute-start | bytes 4718600 | tf_op jit(solution)/shard_map/ppermute | solution.py:45
  (5 other events, 29.4 us)

commit v2 on v1

--- a/solution.py
+++ b/solution.py
@@ -158,7 +158,9 @@
 
         def exchange(rows, steps):
             pieces = [rows[j * chunk : (j + 1) * chunk] for j in range(half)]
-            moved = [to_owner(pieces[j], steps[j]) for j in range(1, half)]
+            moved = []
+            for j in range(1, half):
+                moved.append(to_owner(pieces[j], steps[j]))
             return jnp.concatenate([pieces[0]] + moved, axis=0)
 
         tok_first = [dot(tok_place[0], part) for part in tok_own]
@@ -239,6 +241,7 @@
             other = across(other, mask)
             own = contract_first(sides[0], right_side)
             total = (own + other.astype(jnp.float32)).astype(jnp.bfloat16)
+            total = lax.optimization_barrier(total)
             return jnp.concatenate(turned(total), axis=1)
 
         layer_out = join(weighted, returned, 1)

time: 342 us -> 342 us (level)
  no operation moved by 1% of the time
where the time goes in v2:
time: 342 us; the launch traced here: 340 us
  waiting for transfers between devices  215 us (63%)
  starting transfers between devices  81.2 us (24%)
  matrix products  27.6 us (8%)
  other arithmetic  13.8 us (4%)
    ppermute x41, waiting for transfers between devices, move(): return lax.ppermute(value, AXES, pairs)  175 us
    ppermute x41, starting transfers between devices, move(): return lax.ppermute(value, AXES, pairs)  49.5 us
    ppermute x6, waiting for transfers between devices, transpose(): moved = lax.ppermute(value, AXES, pairs)  39.2 us
    ppermute x6, starting transfers between devices, transpose(): moved = lax.ppermute(value, AXES, pairs)  31.7 us
    dot_general x15, matrix products, dot(): return jnp.dot(left_side, right_side, preferred_element_type=jnp.float32)  10.7 us
    dot_general x11, matrix products, contract_first(): lax.dot_general(left_side, right_side, (((0,), (0,)), ((), ())), preferre...  9.51 us
    dot_general x10, matrix products, contract_last(): lax.dot_general(left_side, right_side, (((1,), (1,)), ((), ())), preferre...  7.35 us
  transfers between devices with their start and end apart: 47, of which 28 were waited for; matrix products, arithmetic and copies ran while one was open for 9% of the time, Pallas kernels for 0%

profile of v2, /device:TPU:13, one launch (start us, length us, event | category | flops | bytes accessed | tf_op | source)
XLA Modules:
  0.0 339.7 jit_solution(5801857372217016763)
XLA Ops:
  2.0 2.3 collective-permute-start
  5.8 4.8 %collective-permute-start.14 = (bf16[1024,768]{1,0:T(8,128)(2,1)}, bf16[1024,768]{1,0:T(8,128)(2,1)S(1)}, u32[]{:S(2)}, u32[]{:S(2)}) collective-permute-start(bf16[1024,768]{1,0:T(8,128)(2,1)} %bitcast.106), channel_id=1, source_target_pairs={{1,16},{3,18},{5,20},{7,22},{9,24},{11,26},{13,28},{15,30},{16,1},... | collective-permute-start | bytes 4718600 | tf_op jit(solution)/shard_map/ppermute | solution.py:45
  10.8 1.6 fusion.5
  13.2 1.9 collective-permute-start.12
  15.1 3.6 %collective-permute-start.10 = (bf16[1024,768]{1,0:T(8,128)(2,1)}, bf16[1024,768]{1,0:T(8,128)(2,1)S(1)}, u32[]{:S(2)}, u32[]{:S(2)}) collective-permute-start(bf16[1024,768]{1,0:T(8,128)(2,1)} %bitcast.107), channel_id=1, source_target_pairs={{1,16},{3,18},{5,20},{7,22},{9,24},{11,26},{13,28},{15,30},{16,1},... | collective-permute-start | bytes 4718600 | tf_op jit(solution)/shard_map/ppermute | solution.py:45
  20.8 1.5 fusion.79
  25.8 7.8 %collective-permute-done.2 = bf16[128,2048]{1,0:T(8,128)(2,1)S(1)} collective-permute-done((bf16[128,2048]{1,0:T(8,128)(2,1)}, bf16[128,2048]{1,0:T(8,128)(2,1)S(1)}, u32[]{:S(2)}, u32[]{:S(2)}) %collective-permute-start.2) | collective-permute-done | bytes 524320 | tf_op jit(solution)/shard_map/ppermute | solution.py:36
  34.8 10.2 %collective-permute-done.25 = bf16[56,2048]{1,0:T(8,128)(2,1)S(1)} collective-permute-done((bf16[56,2048]{1,0:T(8,128)(2,1)S(1)}, bf16[56,2048]{1,0:T(8,128)(2,1)S(1)}, u32[]{:S(2)}, u32[]{:S(2)}) %collective-permute-start.25) | collective-permute-done | bytes 229408 | tf_op jit(solution)/shard_map/ppermute | solution.py:36
  44.9 6.4 %collective-permute-done.26 = bf16[56,2048]{1,0:T(8,128)(2,1)S(1)} collective-permute-done((bf16[56,2048]{1,0:T(8,128)(2,1)S(1)}, bf16[56,2048]{1,0:T(8,128)(2,1)S(1)}, u32[]{:S(2)}, u32[]{:S(2)}) %collective-permute-start.26) | collective-permute-done | bytes 229408 | tf_op jit(solution)/shard_map/ppermute | solution.py:36
  51.7 6.1 %collective-permute-done.27 = bf16[56,2048]{1,0:T(8,128)(2,1)S(1)} collective-permute-done((bf16[56,2048]{1,0:T(8,128)(2,1)S(1)}, bf16[56,2048]{1,0:T(8,128)(2,1)S(1)}, u32[]{:S(2)}, u32[]{:S(2)}) %collective-permute-start.27) | collective-permute-done | bytes 229408 | tf_op jit(solution)/shard_map/ppermute | solution.py:36
  59.1 9.6 %collective-permute-done.28 = bf16[56,2048]{1,0:T(8,128)(2,1)S(1)} collective-permute-done((bf16[56,2048]{1,0:T(8,128)(2,1)S(1)}, bf16[56,2048]{1,0:T(8,128)(2,1)S(1)}, u32[]{:S(2)}, u32[]{:S(2)}) %collective-permute-start.28) | collective-permute-done | bytes 229408 | tf_op jit(solution)/shard_map/ppermute | solution.py:36
  68.7 3.7 %collective-permute-start.29 = (bf16[56,2048]{1,0:T(8,128)(2,1)S(1)}, bf16[56,2048]{1,0:T(8,128)(2,1)S(1)}, u32[]{:S(2)}, u32[]{:S(2)}) collective-permute-start(bf16[56,2048]{1,0:T(8,128)(2,1)S(1)} %get-tuple-element.54), channel_id=1, source_target_pairs={{0,10},{16,26},{2,8},{18,24},{4,14},{20,30},{6,12},{22,28},{8,2},{... | collective-permute-start | bytes 688136 | tf_op jit(solution)/shard_map/ppermute | solution.py:36
  72.5 8.6 %collective-permute-done.29 = bf16[56,2048]{1,0:T(8,128)(2,1)S(1)} collective-permute-done((bf16[56,2048]{1,0:T(8,128)(2,1)S(1)}, bf16[56,2048]{1,0:T(8,128)(2,1)S(1)}, u32[]{:S(2)}, u32[]{:S(2)}) %collective-permute-start.29) | collective-permute-done | bytes 229408 | tf_op jit(solution)/shard_map/ppermute | solution.py:36
  82.1 9.2 %collective-permute-done.30 = bf16[56,2048]{1,0:T(8,128)(2,1)S(1)} collective-permute-done((bf16[56,2048]{1,0:T(8,128)(2,1)S(1)}, bf16[56,2048]{1,0:T(8,128)(2,1)S(1)}, u32[]{:S(2)}, u32[]{:S(2)}) %collective-permute-start.30) | collective-permute-done | bytes 229408 | tf_op jit(solution)/shard_map/ppermute | solution.py:36
  91.3 2.1 collective-permute-start.9
  94.7 10.5 %collective-permute-done.3 = bf16[56,2048]{1,0:T(8,128)(2,1)S(1)} collective-permute-done((bf16[56,2048]{1,0:T(8,128)(2,1)S(1)}, bf16[56,2048]{1,0:T(8,128)(2,1)S(1)}, u32[]{:S(2)}, u32[]{:S(2)}) %collective-permute-start.3) | collective-permute-done | bytes 229408 | tf_op jit(solution)/shard_map/ppermute | solution.py:36
  105.3 6.4 %collective-permute-done.4 = bf16[56,2048]{1,0:T(8,128)(2,1)S(1)} collective-permute-done((bf16[56,2048]{1,0:T(8,128)(2,1)S(1)}, bf16[56,2048]{1,0:T(8,128)(2,1)S(1)}, u32[]{:S(2)}, u32[]{:S(2)}) %collective-permute-start.4) | collective-permute-done | bytes 229408 | tf_op jit(solution)/shard_map/ppermute | solution.py:36
  111.7 6.6 %collective-permute-done.5 = bf16[56,2048]{1,0:T(8,128)(2,1)S(1)} collective-permute-done((bf16[56,2048]{1,0:T(8,128)(2,1)S(1)}, bf16[56,2048]{1,0:T(8,128)(2,1)S(1)}, u32[]{:S(2)}, u32[]{:S(2)}) %collective-permute-start.5) | collective-permute-done | bytes 229408 | tf_op jit(solution)/shard_map/ppermute | solution.py:36
  118.3 4.8 %collective-permute-done.6 = bf16[56,2048]{1,0:T(8,128)(2,1)S(1)} collective-permute-done((bf16[56,2048]{1,0:T(8,128)(2,1)S(1)}, bf16[56,2048]{1,0:T(8,128)(2,1)S(1)}, u32[]{:S(2)}, u32[]{:S(2)}) %collective-permute-start.6) | collective-permute-done | bytes 229408 | tf_op jit(solution)/shard_map/ppermute | solution.py:36
  123.2 1.9 collective-permute-start.7
  125.4 4.9 %collective-permute-start.15 = (bf16[1024,768]{1,0:T(8,128)(2,1)S(1)}, bf16[1024,768]{1,0:T(8,128)(2,1)S(1)}, u32[]{:S(2)}, u32[]{:S(2)}) collective-permute-start(bf16[1024,768]{1,0:T(8,128)(2,1)S(1)} %broadcast_select_fusion.3), channel_id=1, source_target_pairs={{0,1},{16,17},{2,3},{18,19},{4,5},{20,21},{6,7},{22,23},{8,9},{24,... | collective-permute-start | bytes 4718600 | tf_op jit(solution)/shard_map/ppermute | solution.py:36
  130.5 4.1 %collective-permute-start.11 = (bf16[1024,768]{1,0:T(8,128)(2,1)S(1)}, bf16[1024,768]{1,0:T(8,128)(2,1)S(1)}, u32[]{:S(2)}, u32[]{:S(2)}) collective-permute-start(bf16[1024,768]{1,0:T(8,128)(2,1)S(1)} %broadcast_select_fusion.5), channel_id=1, source_target_pairs={{0,1},{16,17},{2,3},{18,19},{4,5},{20,21},{6,7},{22,23},{8,9},{24,... | collective-permute-start | bytes 4718600 | tf_op jit(solution)/shard_map/ppermute | solution.py:36
  136.2 2.4 collective-permute-start.13
  153.5 2.3 collective-permute-start.38
  159.1 8.7 %collective-permute-done.32 = bf16[56,2048]{1,0:T(8,128)(2,1)S(1)} collective-permute-done((bf16[56,2048]{1,0:T(8,128)(2,1)S(1)}, bf16[56,2048]{1,0:T(8,128)(2,1)S(1)}, u32[]{:S(2)}, u32[]{:S(2)}) %collective-permute-start.32) | collective-permute-done | bytes 229408 | tf_op jit(solution)/shard_map/ppermute | solution.py:36
  168.1 6.4 %collective-permute-done.33 = bf16[56,2048]{1,0:T(8,128)(2,1)S(1)} collective-permute-done((bf16[56,2048]{1,0:T(8,128)(2,1)S(1)}, bf16[56,2048]{1,0:T(8,128)(2,1)S(1)}, u32[]{:S(2)}, u32[]{:S(2)}) %collective-permute-start.33) | collective-permute-done | bytes 229408 | tf_op jit(solution)/shard_map/ppermute | solution.py:36
  174.7 6.4 %collective-permute-done.34 = bf16[56,2048]{1,0:T(8,128)(2,1)S(1)} collective-permute-done((bf16[56,2048]{1,0:T(8,128)(2,1)S(1)}, bf16[56,2048]{1,0:T(8,128)(2,1)S(1)}, u32[]{:S(2)}, u32[]{:S(2)}) %collective-permute-start.34) | collective-permute-done | bytes 229408 | tf_op jit(solution)/shard_map/ppermute | solution.py:36
  181.2 4.8 %collective-permute-done.35 = bf16[56,2048]{1,0:T(8,128)(2,1)S(1)} collective-permute-done((bf16[56,2048]{1,0:T(8,128)(2,1)S(1)}, bf16[56,2048]{1,0:T(8,128)(2,1)S(1)}, u32[]{:S(2)}, u32[]{:S(2)}) %collective-permute-start.35) | collective-permute-done | bytes 229408 | tf_op jit(solution)/shard_map/ppermute | solution.py:36
  186.1 1.3 collective-permute-start.36
  187.4 4.4 %collective-permute-done.36 = bf16[56,2048]{1,0:T(8,128)(2,1)S(1)} collective-permute-done((bf16[56,2048]{1,0:T(8,128)(2,1)S(1)}, bf16[56,2048]{1,0:T(8,128)(2,1)S(1)}, u32[]{:S(2)}, u32[]{:S(2)}) %collective-permute-start.36) | collective-permute-done | bytes 229408 | tf_op jit(solution)/shard_map/ppermute | solution.py:36
  192.7 4.9 %collective-permute-done.37 = bf16[56,2048]{1,0:T(8,128)(2,1)S(1)} collective-permute-done((bf16[56,2048]{1,0:T(8,128)(2,1)S(1)}, bf16[56,2048]{1,0:T(8,128)(2,1)S(1)}, u32[]{:S(2)}, u32[]{:S(2)}) %collective-permute-start.37) | collective-permute-done | bytes 229408 | tf_op jit(solution)/shard_map/ppermute | solution.py:36
  197.6 1.8 collective-permute-start.22
  200.7 7.6 %collective-permute-done.16 = bf16[56,2048]{1,0:T(8,128)(2,1)S(1)} collective-permute-done((bf16[56,2048]{1,0:T(8,128)(2,1)S(1)}, bf16[56,2048]{1,0:T(8,128)(2,1)S(1)}, u32[]{:S(2)}, u32[]{:S(2)}) %collective-permute-start.16) | collective-permute-done | bytes 229408 | tf_op jit(solution)/shard_map/ppermute | solution.py:36
  208.4 6.4 %collective-permute-done.17 = bf16[56,2048]{1,0:T(8,128)(2,1)S(1)} collective-permute-done((bf16[56,2048]{1,0:T(8,128)(2,1)S(1)}, bf16[56,2048]{1,0:T(8,128)(2,1)S(1)}, u32[]{:S(2)}, u32[]{:S(2)}) %collective-permute-start.17) | collective-permute-done | bytes 229408 | tf_op jit(solution)/shard_map/ppermute | solution.py:36
  214.8 1.4 collective-permute-start.18
  216.3 6.3 %collective-permute-done.18 = bf16[56,2048]{1,0:T(8,128)(2,1)S(1)} collective-permute-done((bf16[56,2048]{1,0:T(8,128)(2,1)S(1)}, bf16[56,2048]{1,0:T(8,128)(2,1)S(1)}, u32[]{:S(2)}, u32[]{:S(2)}) %collective-permute-start.18) | collective-permute-done | bytes 229408 | tf_op jit(solution)/shard_map/ppermute | solution.py:36
  223.2 7.7 %collective-permute-done.19 = bf16[56,2048]{1,0:T(8,128)(2,1)S(1)} collective-permute-done((bf16[56,2048]{1,0:T(8,128)(2,1)S(1)}, bf16[56,2048]{1,0:T(8,128)(2,1)S(1)}, u32[]{:S(2)}, u32[]{:S(2)}) %collective-permute-start.19) | collective-permute-done | bytes 229408 | tf_op jit(solution)/shard_map/ppermute | solution.py:36
  231.8 8.7 %collective-permute-done.20 = bf16[56,2048]{1,0:T(8,128)(2,1)S(1)} collective-permute-done((bf16[56,2048]{1,0:T(8,128)(2,1)S(1)}, bf16[56,2048]{1,0:T(8,128)(2,1)S(1)}, u32[]{:S(2)}, u32[]{:S(2)}) %collective-permute-start.20) | collective-permute-done | bytes 229408 | tf_op jit(solution)/shard_map/ppermute | solution.py:36
  240.5 4.8 %collective-permute-done.21 = bf16[56,2048]{1,0:T(8,128)(2,1)S(1)} collective-permute-done((bf16[56,2048]{1,0:T(8,128)(2,1)S(1)}, bf16[56,2048]{1,0:T(8,128)(2,1)S(1)}, u32[]{:S(2)}, u32[]{:S(2)}) %collective-permute-start.21) | collective-permute-done | bytes 229408 | tf_op jit(solution)/shard_map/ppermute | solution.py:36
  245.4 8.1 %collective-permute-start.39 = (bf16[128,2048]{1,0:T(8,128)(2,1)S(1)}, bf16[128,2048]{1,0:T(8,128)(2,1)S(1)}, u32[]{:S(2)}, u32[]{:S(2)}) collective-permute-start(bf16[128,2048]{1,0:T(8,128)(2,1)S(1)} %convolution_convert_fusion.2), channel_id=1, source_target_pairs={{0,8},{16,24},{2,10},{18,26},{4,12},{20,28},{6,14},{22,30},{8,0},{... | collective-permute-start | bytes 1572872 | tf_op jit(solution)/shard_map/ppermute | solution.py:36
  257.9 11.0 %collective-permute-done.39 = bf16[128,2048]{1,0:T(8,128)(2,1)S(1)} collective-permute-done((bf16[128,2048]{1,0:T(8,128)(2,1)S(1)}, bf16[128,2048]{1,0:T(8,128)(2,1)S(1)}, u32[]{:S(2)}, u32[]{:S(2)}) %collective-permute-start.39) | collective-permute-done | bytes 524320 | tf_op jit(solution)/shard_map/ppermute | solution.py:36
  269.4 1.3 add_convert_fusion
  270.8 15.8 %collective-permute-start.46 = (bf16[1024,768]{1,0:T(8,128)(2,1)S(1)}, bf16[1024,768]{1,0:T(8,128)(2,1)S(1)}, u32[]{:S(2)}, u32[]{:S(2)}) collective-permute-start(bf16[1024,768]{1,0:T(8,128)(2,1)S(1)} %add_convert_fusion), channel_id=1, source_target_pairs={{1,16},{3,18},{5,20},{7,22},{9,24},{11,26},{13,28},{15,30},{16,1},... | collective-permute-start | bytes 4718600 | tf_op jit(solution)/shard_map/ppermute | solution.py:45
  287.6 1.9 collective-permute-start.44
  290.6 3.6 %collective-permute-start.42 = (bf16[1024,768]{1,0:T(8,128)(2,1)S(1)}, bf16[1024,768]{1,0:T(8,128)(2,1)S(1)}, u32[]{:S(2)}, u32[]{:S(2)}) collective-permute-start(bf16[1024,768]{1,0:T(8,128)(2,1)S(1)} %add_convert_fusion.2), channel_id=1, source_target_pairs={{1,16},{3,18},{5,20},{7,22},{9,24},{11,26},{13,28},{15,30},{16,1},... | collective-permute-start | bytes 4718600 | tf_op jit(solution)/shard_map/ppermute | solution.py:45
  296.5 8.1 %collective-permute-done.46 = bf16[1024,768]{1,0:T(8,128)(2,1)S(1)} collective-permute-done((bf16[1024,768]{1,0:T(8,128)(2,1)S(1)}, bf16[1024,768]{1,0:T(8,128)(2,1)S(1)}, u32[]{:S(2)}, u32[]{:S(2)}) %collective-permute-start.46) | collective-permute-done | bytes 1572896 | tf_op jit(solution)/shard_map/ppermute | solution.py:45
  306.0 15.5 %collective-permute-done.44 = bf16[1024,768]{1,0:T(8,128)(2,1)S(1)} collective-permute-done((bf16[1024,768]{1,0:T(8,128)(2,1)S(1)}, bf16[1024,768]{1,0:T(8,128)(2,1)S(1)}, u32[]{:S(2)}, u32[]{:S(2)}) %collective-permute-start.44) | collective-permute-done | bytes 1572896 | tf_op jit(solution)/shard_map/ppermute | solution.py:45
  322.8 15.5 %collective-permute-done.42 = bf16[1024,768]{1,0:T(8,128)(2,1)S(1)} collective-permute-done((bf16[1024,768]{1,0:T(8,128)(2,1)S(1)}, bf16[1024,768]{1,0:T(8,128)(2,1)S(1)}, u32[]{:S(2)}, u32[]{:S(2)}) %collective-permute-start.42) | collective-permute-done | bytes 1572896 | tf_op jit(solution)/shard_map/ppermute | solution.py:45
  (162 shorter events, 52.1 us)
Async XLA Ops:
  2.0 13.1 %collective-permute-start = (f32[4,128]{1,0:T(4,128)S(1)}, f32[4,128]{1,0:T(4,128)S(1)}, u32[]{:S(2)}, u32[]{:S(2)}) collective-permute-start(f32[4,128]{1,0:T(4,128)S(1)} %get-tuple-element.95), channel_id=1, source_target_pairs={{0,8},{16,24},{2,10},{18,26},{4,12},{20,28},{6,14},{22,30},{8,0},{... | collective-permute-start | bytes 6152 | tf_op jit(solution)/shard_map/ppermute | solution.py:36
  4.3 8.9 %collective-permute-start.1 = (f32[4,128]{1,0:T(4,128)S(1)}, f32[4,128]{1,0:T(4,128)S(1)}, u32[]{:S(2)}, u32[]{:S(2)}) collective-permute-start(f32[4,128]{1,0:T(4,128)S(1)} %get-tuple-element.95), channel_id=1, source_target_pairs={{0,16},{16,0},{2,18},{18,2},{4,20},{20,4},{6,22},{22,6},{8,24},{24... | collective-permute-start | bytes 6152 | tf_op jit(solution)/shard_map/ppermute | solution.py:36
  5.5 28.1 %collective-permute-start.2 = (bf16[128,2048]{1,0:T(8,128)(2,1)}, bf16[128,2048]{1,0:T(8,128)(2,1)S(1)}, u32[]{:S(2)}, u32[]{:S(2)}) collective-permute-start(bf16[128,2048]{1,0:T(8,128)(2,1)} %param.15), channel_id=1, source_target_pairs={{0,8},{16,24},{2,10},{18,26},{4,12},{20,28},{6,14},{22,30},{8,0},{... | collective-permute-start | bytes 1572872 | tf_op jit(solution)/shard_map/ppermute | solution.py:36
  5.6 17.9 %collective-permute-start.24 = (bf16[128,2048]{1,0:T(8,128)(2,1)}, bf16[128,2048]{1,0:T(8,128)(2,1)S(1)}, u32[]{:S(2)}, u32[]{:S(2)}) collective-permute-start(bf16[128,2048]{1,0:T(8,128)(2,1)} %param.22), channel_id=1, source_target_pairs={{0,16},{16,0},{2,18},{18,2},{4,20},{20,4},{6,22},{22,6},{8,24},{24... | collective-permute-start | bytes 1572872 | tf_op jit(solution)/shard_map/ppermute | solution.py:36
  5.8 119.2 %collective-permute-start.14 = (bf16[1024,768]{1,0:T(8,128)(2,1)}, bf16[1024,768]{1,0:T(8,128)(2,1)S(1)}, u32[]{:S(2)}, u32[]{:S(2)}) collective-permute-start(bf16[1024,768]{1,0:T(8,128)(2,1)} %bitcast.106), channel_id=1, source_target_pairs={{1,16},{3,18},{5,20},{7,22},{9,24},{11,26},{13,28},{15,30},{16,1},... | collective-permute-start | bytes 4718600 | tf_op jit(solution)/shard_map/ppermute | solution.py:45
  13.2 122.6 %collective-permute-start.12 = (bf16[1024,768]{1,0:T(8,128)(2,1)}, bf16[1024,768]{1,0:T(8,128)(2,1)S(1)}, u32[]{:S(2)}, u32[]{:S(2)}) collective-permute-start(bf16[1024,768]{1,0:T(8,128)(2,1)} %bitcast.108), channel_id=1, source_target_pairs={{1,16},{3,18},{5,20},{7,22},{9,24},{11,26},{13,28},{15,30},{16,1},... | collective-permute-start | bytes 4718600 | tf_op jit(solution)/shard_map/ppermute | solution.py:45
  15.1 110.2 %collective-permute-start.10 = (bf16[1024,768]{1,0:T(8,128)(2,1)}, bf16[1024,768]{1,0:T(8,128)(2,1)S(1)}, u32[]{:S(2)}, u32[]{:S(2)}) collective-permute-start(bf16[1024,768]{1,0:T(8,128)(2,1)} %bitcast.107), channel_id=1, source_target_pairs={{1,16},{3,18},{5,20},{7,22},{9,24},{11,26},{13,28},{15,30},{16,1},... | collective-permute-start | bytes 4718600 | tf_op jit(solution)/shard_map/ppermute | solution.py:45
  24.5 69.0 %collective-permute-start.31 = (bf16[56,2048]{1,0:T(8,128)(2,1)S(1)}, bf16[56,2048]{1,0:T(8,128)(2,1)S(1)}, u32[]{:S(2)}, u32[]{:S(2)}) collective-permute-start(bf16[56,2048]{1,0:T(8,128)(2,1)S(1)} %get-tuple-element.48), channel_id=1, source_target_pairs={{0,14},{16,30},{2,12},{18,28},{4,10},{20,26},{6,8},{22,24},{8,6},{... | collective-permute-start | bytes 688136 | tf_op jit(solution)/shard_map/ppermute | solution.py:36
  33.6 11.3 %collective-permute-start.25 = (bf16[56,2048]{1,0:T(8,128)(2,1)S(1)}, bf16[56,2048]{1,0:T(8,128)(2,1)S(1)}, u32[]{:S(2)}, u32[]{:S(2)}) collective-permute-start(bf16[56,2048]{1,0:T(8,128)(2,1)S(1)} %get-tuple-element.50), channel_id=1, source_target_pairs={{0,2},{16,18},{2,0},{18,16},{4,6},{20,22},{6,4},{22,20},{8,10},{24... | collective-permute-start | bytes 688136 | tf_op jit(solution)/shard_map/ppermute | solution.py:36
  44.9 6.4 %collective-permute-start.26 = (bf16[56,2048]{1,0:T(8,128)(2,1)S(1)}, bf16[56,2048]{1,0:T(8,128)(2,1)S(1)}, u32[]{:S(2)}, u32[]{:S(2)}) collective-permute-start(bf16[56,2048]{1,0:T(8,128)(2,1)S(1)} %get-tuple-element.51), channel_id=1, source_target_pairs={{0,4},{16,20},{2,6},{18,22},{4,0},{20,16},{6,2},{22,18},{8,12},{24... | collective-permute-start | bytes 688136 | tf_op jit(solution)/shard_map/ppermute | solution.py:36
  51.4 6.5 %collective-permute-start.27 = (bf16[56,2048]{1,0:T(8,128)(2,1)S(1)}, bf16[56,2048]{1,0:T(8,128)(2,1)S(1)}, u32[]{:S(2)}, u32[]{:S(2)}) collective-permute-start(bf16[56,2048]{1,0:T(8,128)(2,1)S(1)} %get-tuple-element.52), channel_id=1, source_target_pairs={{0,6},{16,22},{2,4},{18,20},{4,2},{20,18},{6,0},{22,16},{8,14},{24... | collective-permute-start | bytes 688136 | tf_op jit(solution)/shard_map/ppermute | solution.py:36
  57.8 10.9 %collective-permute-start.28 = (bf16[56,2048]{1,0:T(8,128)(2,1)S(1)}, bf16[56,2048]{1,0:T(8,128)(2,1)S(1)}, u32[]{:S(2)}, u32[]{:S(2)}) collective-permute-start(bf16[56,2048]{1,0:T(8,128)(2,1)S(1)} %get-tuple-element.53), channel_id=1, source_target_pairs={{0,8},{16,24},{2,10},{18,26},{4,12},{20,28},{6,14},{22,30},{8,0},{... | collective-permute-start | bytes 688136 | tf_op jit(solution)/shard_map/ppermute | solution.py:36
  68.7 56.4 %copy-start = (bf16[1,1024,768]{2,1,0:T(8,128)(2,1)S(1)}, bf16[1,1024,768]{2,1,0:T(8,128)(2,1)}, u32[]{:S(2)}) copy-start(bf16[1,1024,768]{2,1,0:T(8,128)(2,1)} %param.21) | copy-start | bytes 4718596
  68.7 12.3 %collective-permute-start.29 = (bf16[56,2048]{1,0:T(8,128)(2,1)S(1)}, bf16[56,2048]{1,0:T(8,128)(2,1)S(1)}, u32[]{:S(2)}, u32[]{:S(2)}) collective-permute-start(bf16[56,2048]{1,0:T(8,128)(2,1)S(1)} %get-tuple-element.54), channel_id=1, source_target_pairs={{0,10},{16,26},{2,8},{18,24},{4,14},{20,30},{6,12},{22,28},{8,2},{... | collective-permute-start | bytes 688136 | tf_op jit(solution)/shard_map/ppermute | solution.py:36
  81.1 10.3 %collective-permute-start.30 = (bf16[56,2048]{1,0:T(8,128)(2,1)S(1)}, bf16[56,2048]{1,0:T(8,128)(2,1)S(1)}, u32[]{:S(2)}, u32[]{:S(2)}) collective-permute-start(bf16[56,2048]{1,0:T(8,128)(2,1)S(1)} %get-tuple-element.55), channel_id=1, source_target_pairs={{0,12},{16,28},{2,14},{18,30},{4,8},{20,24},{6,10},{22,26},{8,4},{... | collective-permute-start | bytes 688136 | tf_op jit(solution)/shard_map/ppermute | solution.py:36
  91.3 47.2 %collective-permute-start.9 = (bf16[56,2048]{1,0:T(8,128)(2,1)S(1)}, bf16[56,2048]{1,0:T(8,128)(2,1)S(1)}, u32[]{:S(2)}, u32[]{:S(2)}) collective-permute-start(bf16[56,2048]{1,0:T(8,128)(2,1)S(1)} %get-tuple-element.64), channel_id=1, source_target_pairs={{0,22},{16,6},{2,20},{18,4},{4,18},{20,2},{6,16},{22,0},{8,30},{24... | collective-permute-start | bytes 688136 | tf_op jit(solution)/shard_map/ppermute | solution.py:36
  93.5 11.7 %collective-permute-start.3 = (bf16[56,2048]{1,0:T(8,128)(2,1)S(1)}, bf16[56,2048]{1,0:T(8,128)(2,1)S(1)}, u32[]{:S(2)}, u32[]{:S(2)}) collective-permute-start(bf16[56,2048]{1,0:T(8,128)(2,1)S(1)} %get-tuple-element.66), channel_id=1, source_target_pairs={{0,16},{16,0},{2,18},{18,2},{4,20},{20,4},{6,22},{22,6},{8,24},{24... | collective-permute-start | bytes 688136 | tf_op jit(solution)/shard_map/ppermute | solution.py:36
  105.2 6.5 %collective-permute-start.4 = (bf16[56,2048]{1,0:T(8,128)(2,1)S(1)}, bf16[56,2048]{1,0:T(8,128)(2,1)S(1)}, u32[]{:S(2)}, u32[]{:S(2)}) collective-permute-start(bf16[56,2048]{1,0:T(8,128)(2,1)S(1)} %get-tuple-element.67), channel_id=1, source_target_pairs={{0,2},{16,18},{2,0},{18,16},{4,6},{20,22},{6,4},{22,20},{8,10},{24... | collective-permute-start | bytes 688136 | tf_op jit(solution)/shard_map/ppermute | solution.py:36
  111.7 6.6 %collective-permute-start.5 = (bf16[56,2048]{1,0:T(8,128)(2,1)S(1)}, bf16[56,2048]{1,0:T(8,128)(2,1)S(1)}, u32[]{:S(2)}, u32[]{:S(2)}) collective-permute-start(bf16[56,2048]{1,0:T(8,128)(2,1)S(1)} %get-tuple-element.68), channel_id=1, source_target_pairs={{0,18},{16,2},{2,16},{18,0},{4,22},{20,6},{6,20},{22,4},{8,26},{24... | collective-permute-start | bytes 688136 | tf_op jit(solution)/shard_map/ppermute | solution.py:36
  118.3 4.9 %collective-permute-start.6 = (bf16[56,2048]{1,0:T(8,128)(2,1)S(1)}, bf16[56,2048]{1,0:T(8,128)(2,1)S(1)}, u32[]{:S(2)}, u32[]{:S(2)}) collective-permute-start(bf16[56,2048]{1,0:T(8,128)(2,1)S(1)} %get-tuple-element.69), channel_id=1, source_target_pairs={{0,4},{16,20},{2,6},{18,22},{4,0},{20,16},{6,2},{22,18},{8,12},{24... | collective-permute-start | bytes 688136 | tf_op jit(solution)/shard_map/ppermute | solution.py:36
  123.2 7.3 %collective-permute-start.7 = (bf16[56,2048]{1,0:T(8,128)(2,1)S(1)}, bf16[56,2048]{1,0:T(8,128)(2,1)S(1)}, u32[]{:S(2)}, u32[]{:S(2)}) collective-permute-start(bf16[56,2048]{1,0:T(8,128)(2,1)S(1)} %get-tuple-element.70), channel_id=1, source_target_pairs={{0,20},{16,4},{2,22},{18,6},{4,16},{20,0},{6,18},{22,2},{8,28},{24... | collective-permute-start | bytes 688136 | tf_op jit(solution)/shard_map/ppermute | solution.py:36
  125.1 9.5 %collective-permute-start.8 = (bf16[56,2048]{1,0:T(8,128)(2,1)S(1)}, bf16[56,2048]{1,0:T(8,128)(2,1)S(1)}, u32[]{:S(2)}, u32[]{:S(2)}) collective-permute-start(bf16[56,2048]{1,0:T(8,128)(2,1)S(1)} %get-tuple-element.71), channel_id=1, source_target_pairs={{0,6},{16,22},{2,4},{18,20},{4,2},{20,18},{6,0},{22,16},{8,14},{24... | collective-permute-start | bytes 688136 | tf_op jit(solution)/shard_map/ppermute | solution.py:36
  125.4 13.2 %collective-permute-start.15 = (bf16[1024,768]{1,0:T(8,128)(2,1)S(1)}, bf16[1024,768]{1,0:T(8,128)(2,1)S(1)}, u32[]{:S(2)}, u32[]{:S(2)}) collective-permute-start(bf16[1024,768]{1,0:T(8,128)(2,1)S(1)} %broadcast_select_fusion.3), channel_id=1, source_target_pairs={{0,1},{16,17},{2,3},{18,19},{4,5},{20,21},{6,7},{22,23},{8,9},{24,... | collective-permute-start | bytes 4718600 | tf_op jit(solution)/shard_map/ppermute | solution.py:36
  130.5 9.0 %collective-permute-start.11 = (bf16[1024,768]{1,0:T(8,128)(2,1)S(1)}, bf16[1024,768]{1,0:T(8,128)(2,1)S(1)}, u32[]{:S(2)}, u32[]{:S(2)}) collective-permute-start(bf16[1024,768]{1,0:T(8,128)(2,1)S(1)} %broadcast_select_fusion.5), channel_id=1, source_target_pairs={{0,1},{16,17},{2,3},{18,19},{4,5},{20,21},{6,7},{22,23},{8,9},{24,... | collective-permute-start | bytes 4718600 | tf_op jit(solution)/shard_map/ppermute | solution.py:36
  136.2 6.0 %collective-permute-start.13 = (bf16[1024,768]{1,0:T(8,128)(2,1)S(1)}, bf16[1024,768]{1,0:T(8,128)(2,1)S(1)}, u32[]{:S(2)}, u32[]{:S(2)}) collective-permute-start(bf16[1024,768]{1,0:T(8,128)(2,1)S(1)} %broadcast_select_fusion.4), channel_id=1, source_target_pairs={{0,1},{16,17},{2,3},{18,19},{4,5},{20,21},{6,7},{22,23},{8,9},{24,... | collective-permute-start | bytes 4718600 | tf_op jit(solution)/shard_map/ppermute | solution.py:36
  150.9 118.6 %collective-permute-start.45 = (bf16[1024,768]{1,0:T(8,128)(2,1)S(1)}, bf16[1024,768]{1,0:T(8,128)(2,1)S(1)}, u32[]{:S(2)}, u32[]{:S(2)}) collective-permute-start(bf16[1024,768]{1,0:T(8,128)(2,1)S(1)} %convolution_convert_fusion.4), channel_id=1, source_target_pairs={{0,1},{16,17},{2,3},{18,19},{4,5},{20,21},{6,7},{22,23},{8,9},{24,... | collective-permute-start | bytes 4718600 | tf_op jit(solution)/shard_map/ppermute | solution.py:36
  151.0 135.6 %collective-permute-start.43 = (bf16[1024,768]{1,0:T(8,128)(2,1)S(1)}, bf16[1024,768]{1,0:T(8,128)(2,1)S(1)}, u32[]{:S(2)}, u32[]{:S(2)}) collective-permute-start(bf16[1024,768]{1,0:T(8,128)(2,1)S(1)} %convolution_convert_fusion.5), channel_id=1, source_target_pairs={{0,1},{16,17},{2,3},{18,19},{4,5},{20,21},{6,7},{22,23},{8,9},{24,... | collective-permute-start | bytes 4718600 | tf_op jit(solution)/shard_map/ppermute | solution.py:36
  151.4 138.1 %collective-permute-start.41 = (bf16[1024,768]{1,0:T(8,128)(2,1)S(1)}, bf16[1024,768]{1,0:T(8,128)(2,1)S(1)}, u32[]{:S(2)}, u32[]{:S(2)}) collective-permute-start(bf16[1024,768]{1,0:T(8,128)(2,1)S(1)} %convolution_convert_fusion.6), channel_id=1, source_target_pairs={{0,1},{16,17},{2,3},{18,19},{4,5},{20,21},{6,7},{22,23},{8,9},{24,... | collective-permute-start | bytes 4718600 | tf_op jit(solution)/shard_map/ppermute | solution.py:36
  153.5 46.0 %collective-permute-start.38 = (bf16[56,2048]{1,0:T(8,128)(2,1)S(1)}, bf16[56,2048]{1,0:T(8,128)(2,1)S(1)}, u32[]{:S(2)}, u32[]{:S(2)}) collective-permute-start(bf16[56,2048]{1,0:T(8,128)(2,1)S(1)} %get-tuple-element.40), channel_id=1, source_target_pairs={{0,22},{16,6},{2,20},{18,4},{4,18},{20,2},{6,16},{22,0},{8,30},{24... | collective-permute-start | bytes 688136 | tf_op jit(solution)/shard_map/ppermute | solution.py:36
  155.8 12.0 %collective-permute-start.32 = (bf16[56,2048]{1,0:T(8,128)(2,1)S(1)}, bf16[56,2048]{1,0:T(8,128)(2,1)S(1)}, u32[]{:S(2)}, u32[]{:S(2)}) collective-permute-start(bf16[56,2048]{1,0:T(8,128)(2,1)S(1)} %get-tuple-element.42), channel_id=1, source_target_pairs={{0,16},{16,0},{2,18},{18,2},{4,20},{20,4},{6,22},{22,6},{8,24},{24... | collective-permute-start | bytes 688136 | tf_op jit(solution)/shard_map/ppermute | solution.py:36
  167.8 6.7 %collective-permute-start.33 = (bf16[56,2048]{1,0:T(8,128)(2,1)S(1)}, bf16[56,2048]{1,0:T(8,128)(2,1)S(1)}, u32[]{:S(2)}, u32[]{:S(2)}) collective-permute-start(bf16[56,2048]{1,0:T(8,128)(2,1)S(1)} %get-tuple-element.43), channel_id=1, source_target_pairs={{0,2},{16,18},{2,0},{18,16},{4,6},{20,22},{6,4},{22,20},{8,10},{24... | collective-permute-start | bytes 688136 | tf_op jit(solution)/shard_map/ppermute | solution.py:36
  174.5 6.7 %collective-permute-start.34 = (bf16[56,2048]{1,0:T(8,128)(2,1)S(1)}, bf16[56,2048]{1,0:T(8,128)(2,1)S(1)}, u32[]{:S(2)}, u32[]{:S(2)}) collective-permute-start(bf16[56,2048]{1,0:T(8,128)(2,1)S(1)} %get-tuple-element.44), channel_id=1, source_target_pairs={{0,18},{16,2},{2,16},{18,0},{4,22},{20,6},{6,20},{22,4},{8,26},{24... | collective-permute-start | bytes 688136 | tf_op jit(solution)/shard_map/ppermute | solution.py:36
  181.2 4.9 %collective-permute-start.35 = (bf16[56,2048]{1,0:T(8,128)(2,1)S(1)}, bf16[56,2048]{1,0:T(8,128)(2,1)S(1)}, u32[]{:S(2)}, u32[]{:S(2)}) collective-permute-start(bf16[56,2048]{1,0:T(8,128)(2,1)S(1)} %get-tuple-element.45), channel_id=1, source_target_pairs={{0,4},{16,20},{2,6},{18,22},{4,0},{20,16},{6,2},{22,18},{8,12},{24... | collective-permute-start | bytes 688136 | tf_op jit(solution)/shard_map/ppermute | solution.py:36
  186.1 5.8 %collective-permute-start.36 = (bf16[56,2048]{1,0:T(8,128)(2,1)S(1)}, bf16[56,2048]{1,0:T(8,128)(2,1)S(1)}, u32[]{:S(2)}, u32[]{:S(2)}) collective-permute-start(bf16[56,2048]{1,0:T(8,128)(2,1)S(1)} %get-tuple-element.46), channel_id=1, source_target_pairs={{0,20},{16,4},{2,22},{18,6},{4,16},{20,0},{6,18},{22,2},{8,28},{24... | collective-permute-start | bytes 688136 | tf_op jit(solution)/shard_map/ppermute | solution.py:36
  191.8 5.8 %collective-permute-start.37 = (bf16[56,2048]{1,0:T(8,128)(2,1)S(1)}, bf16[56,2048]{1,0:T(8,128)(2,1)S(1)}, u32[]{:S(2)}, u32[]{:S(2)}) collective-permute-start(bf16[56,2048]{1,0:T(8,128)(2,1)S(1)} %get-tuple-element.47), channel_id=1, source_target_pairs={{0,6},{16,22},{2,4},{18,20},{4,2},{20,18},{6,0},{22,16},{8,14},{24... | collective-permute-start | bytes 688136 | tf_op jit(solution)/shard_map/ppermute | solution.py:36
  197.6 55.9 %collective-permute-start.22 = (bf16[56,2048]{1,0:T(8,128)(2,1)S(1)}, bf16[56,2048]{1,0:T(8,128)(2,1)S(1)}, u32[]{:S(2)}, u32[]{:S(2)}) collective-permute-start(bf16[56,2048]{1,0:T(8,128)(2,1)S(1)} %get-tuple-element.56), channel_id=1, source_target_pairs={{0,14},{16,30},{2,12},{18,28},{4,10},{20,26},{6,8},{22,24},{8,6},{... | collective-permute-start | bytes 688136 | tf_op jit(solution)/shard_map/ppermute | solution.py:36
  199.5 8.8 %collective-permute-start.16 = (bf16[56,2048]{1,0:T(8,128)(2,1)S(1)}, bf16[56,2048]{1,0:T(8,128)(2,1)S(1)}, u32[]{:S(2)}, u32[]{:S(2)}) collective-permute-start(bf16[56,2048]{1,0:T(8,128)(2,1)S(1)} %get-tuple-element.62), channel_id=1, source_target_pairs={{0,2},{16,18},{2,0},{18,16},{4,6},{20,22},{6,4},{22,20},{8,10},{24... | collective-permute-start | bytes 688136 | tf_op jit(solution)/shard_map/ppermute | solution.py:36
  208.3 6.5 %collective-permute-start.17 = (bf16[56,2048]{1,0:T(8,128)(2,1)S(1)}, bf16[56,2048]{1,0:T(8,128)(2,1)S(1)}, u32[]{:S(2)}, u32[]{:S(2)}) collective-permute-start(bf16[56,2048]{1,0:T(8,128)(2,1)S(1)} %get-tuple-element.61), channel_id=1, source_target_pairs={{0,4},{16,20},{2,6},{18,22},{4,0},{20,16},{6,2},{22,18},{8,12},{24... | collective-permute-start | bytes 688136 | tf_op jit(solution)/shard_map/ppermute | solution.py:36
  214.8 7.7 %collective-permute-start.18 = (bf16[56,2048]{1,0:T(8,128)(2,1)S(1)}, bf16[56,2048]{1,0:T(8,128)(2,1)S(1)}, u32[]{:S(2)}, u32[]{:S(2)}) collective-permute-start(bf16[56,2048]{1,0:T(8,128)(2,1)S(1)} %get-tuple-element.60), channel_id=1, source_target_pairs={{0,6},{16,22},{2,4},{18,20},{4,2},{20,18},{6,0},{22,16},{8,14},{24... | collective-permute-start | bytes 688136 | tf_op jit(solution)/shard_map/ppermute | solution.py:36
  222.5 8.4 %collective-permute-start.19 = (bf16[56,2048]{1,0:T(8,128)(2,1)S(1)}, bf16[56,2048]{1,0:T(8,128)(2,1)S(1)}, u32[]{:S(2)}, u32[]{:S(2)}) collective-permute-start(bf16[56,2048]{1,0:T(8,128)(2,1)S(1)} %get-tuple-element.59), channel_id=1, source_target_pairs={{0,8},{16,24},{2,10},{18,26},{4,12},{20,28},{6,14},{22,30},{8,0},{... | collective-permute-start | bytes 688136 | tf_op jit(solution)/shard_map/ppermute | solution.py:36
  230.9 9.6 %collective-permute-start.20 = (bf16[56,2048]{1,0:T(8,128)(2,1)S(1)}, bf16[56,2048]{1,0:T(8,128)(2,1)S(1)}, u32[]{:S(2)}, u32[]{:S(2)}) collective-permute-start(bf16[56,2048]{1,0:T(8,128)(2,1)S(1)} %get-tuple-element.58), channel_id=1, source_target_pairs={{0,10},{16,26},{2,8},{18,24},{4,14},{20,30},{6,12},{22,28},{8,2},{... | collective-permute-start | bytes 688136 | tf_op jit(solution)/shard_map/ppermute | solution.py:36
  240.5 4.9 %collective-permute-start.21 = (bf16[56,2048]{1,0:T(8,128)(2,1)S(1)}, bf16[56,2048]{1,0:T(8,128)(2,1)S(1)}, u32[]{:S(2)}, u32[]{:S(2)}) collective-permute-start(bf16[56,2048]{1,0:T(8,128)(2,1)S(1)} %get-tuple-element.57), channel_id=1, source_target_pairs={{0,12},{16,28},{2,14},{18,30},{4,8},{20,24},{6,10},{22,26},{8,4},{... | collective-permute-start | bytes 688136 | tf_op jit(solution)/shard_map/ppermute | solution.py:36
  245.4 23.6 %collective-permute-start.39 = (bf16[128,2048]{1,0:T(8,128)(2,1)S(1)}, bf16[128,2048]{1,0:T(8,128)(2,1)S(1)}, u32[]{:S(2)}, u32[]{:S(2)}) collective-permute-start(bf16[128,2048]{1,0:T(8,128)(2,1)S(1)} %convolution_convert_fusion.2), channel_id=1, source_target_pairs={{0,8},{16,24},{2,10},{18,26},{4,12},{20,28},{6,14},{22,30},{8,0},{... | collective-permute-start | bytes 1572872 | tf_op jit(solution)/shard_map/ppermute | solution.py:36
  254.4 2.5 collective-permute-start.40
  256.9 37.4 %collective-permute-start.23 = (bf16[128,2048]{1,0:T(8,128)(2,1)S(1)}, bf16[128,2048]{1,0:T(8,128)(2,1)S(1)}, u32[]{:S(2)}, u32[]{:S(2)}) collective-permute-start(bf16[128,2048]{1,0:T(8,128)(2,1)S(1)} %convolution_convert_fusion.3), channel_id=1, source_target_pairs={{0,16},{16,0},{2,18},{18,2},{4,20},{20,4},{6,22},{22,6},{8,24},{24... | collective-permute-start | bytes 1572872 | tf_op jit(solution)/shard_map/ppermute | solution.py:36
  270.8 33.9 %collective-permute-start.46 = (bf16[1024,768]{1,0:T(8,128)(2,1)S(1)}, bf16[1024,768]{1,0:T(8,128)(2,1)S(1)}, u32[]{:S(2)}, u32[]{:S(2)}) collective-permute-start(bf16[1024,768]{1,0:T(8,128)(2,1)S(1)} %add_convert_fusion), channel_id=1, source_target_pairs={{1,16},{3,18},{5,20},{7,22},{9,24},{11,26},{13,28},{15,30},{16,1},... | collective-permute-start | bytes 4718600 | tf_op jit(solution)/shard_map/ppermute | solution.py:45
  287.6 33.9 %collective-permute-start.44 = (bf16[1024,768]{1,0:T(8,128)(2,1)S(1)}, bf16[1024,768]{1,0:T(8,128)(2,1)S(1)}, u32[]{:S(2)}, u32[]{:S(2)}) collective-permute-start(bf16[1024,768]{1,0:T(8,128)(2,1)S(1)} %add_convert_fusion.1), channel_id=1, source_target_pairs={{1,16},{3,18},{5,20},{7,22},{9,24},{11,26},{13,28},{15,30},{16,1},... | collective-permute-start | bytes 4718600 | tf_op jit(solution)/shard_map/ppermute | solution.py:45
  290.6 47.7 %collective-permute-start.42 = (bf16[1024,768]{1,0:T(8,128)(2,1)S(1)}, bf16[1024,768]{1,0:T(8,128)(2,1)S(1)}, u32[]{:S(2)}, u32[]{:S(2)}) collective-permute-start(bf16[1024,768]{1,0:T(8,128)(2,1)S(1)} %add_convert_fusion.2), channel_id=1, source_target_pairs={{1,16},{3,18},{5,20},{7,22},{9,24},{11,26},{13,28},{15,30},{16,1},... | collective-permute-start | bytes 4718600 | tf_op jit(solution)/shard_map/ppermute | solution.py:45
  (5 other events, 29.4 us)
